TPU v7x, 32 devices: a whole 2x2x4 slice. The times are simulated.
32 devices in a mesh: dp: 8 (over y, x, core), mp: 4 (over z).
Axes of the slice: x: 2, y: 2, z: 4, core: 2. Of those that a mesh axis runs over, the one named last changes fastest.
Arguments:
- tokens: bfloat16 [16384, 1280], P(('dp', 'mp')), may hold values from -6 to 6
- segments: int32 [8, 2048], P('dp'), may hold values from 0 to 15, never falling along the last dimension, each value on 1 to 1024 neighbouring positions
- w_query: bfloat16 [1280, 1280], P('dp', 'mp'), may hold values from -0.15625 to 0.15625
- w_key: bfloat16 [1280, 1280], P('dp', 'mp'), may hold values from -0.15625 to 0.15625
- w_value: bfloat16 [1280, 1280], P('dp', 'mp'), may hold values from -0.15625 to 0.15625
- w_output: bfloat16 [1280, 1280], P('mp', 'dp'), may hold values from -1.25 to 1.25
- w_up: bfloat16 [1280, 1280], P('dp', 'mp'), may hold values from -0.15625 to 0.15625
- b_up: float32 [1280], P('mp'), may hold values from -3 to 3
- w_down: bfloat16 [1280, 1280], P('mp', 'dp'), may hold values from -0.25 to 0.25
- b_down: float32 [1280], replicated, may hold values from -3 to 3
- gain_attn: float32 [1280], replicated, may hold values from 0.5 to 1.5
- gain_mlp: float32 [1280], replicated, may hold values from 0.5 to 1.5
- query_scale: float32 [80], replicated, may hold values from -0.5 to 1
- cotangent: bfloat16 [16384, 1280], P(('dp', 'mp')), may hold values from -6 to 6
Outputs:
- layer_out: bfloat16 [16384, 1280], P(('dp', 'mp'))
- tokens_grad: bfloat16 [16384, 1280], P(('dp', 'mp'))
- grad_w_query: float32 [1280, 1280], P('dp', 'mp')
- grad_w_key: float32 [1280, 1280], P('dp', 'mp')
- grad_w_value: float32 [1280, 1280], P('dp', 'mp')
- grad_w_output: float32 [1280, 1280], P('mp', 'dp')
- grad_w_up: float32 [1280, 1280], P('dp', 'mp')
- grad_b_up: float32 [1280], P('mp')
- grad_w_down: float32 [1280, 1280], P('mp', 'dp')
- grad_b_down: float32 [1280], replicated
- grad_gain_attn: float32 [1280], replicated
- grad_gain_mlp: float32 [1280], replicated
- grad_query_scale: float32 [80], replicated
Inputs may be any that keep to these rules, and one draw needn't show every extreme that they name: `segments`: within a sequence segment numbers never fall; documents are 1 to 1024 tokens long.
All inputs are finite; a program needn't handle non-finite values.
Results may differ from a plain program's by a relative error of at most 0.014.
Values may be sent and summed in bfloat16 or wider, within the bound.
A program may use at most 192 MiB of HBM per device.

v0:
```python
import math

import jax
import jax.numpy as jnp
from jax import lax
from jax.sharding import PartitionSpec as P

D = 1280
HD = 80


EPSILON = 1e-06
LOG2E = 1.442695
far_below = -1e30


def row_inverse(values):
    return lax.rsqrt(jnp.mean(values * values, axis=1, keepdims=True) + EPSILON)


def all_rows(values):
    return lax.all_gather(values, "mp", axis=0, tiled=True)


def combine(values):
    return lax.psum_scatter(values, "mp", scatter_dimension=0, tiled=True)


def block_scores(query_block, keys, seg, start, rows):
    length = keys.shape[0]
    scores = jnp.einsum("qhd,khd->hqk", query_block, keys, preferred_element_type=jnp.float32)
    pos_query = start + jnp.arange(rows, dtype=jnp.int32)
    pos_key = jnp.arange(length, dtype=jnp.int32)
    seg_query = lax.dynamic_slice_in_dim(seg, start, rows, 0)
    allowed = (pos_query[:, None] >= pos_key[None, :]) & (seg_query[:, None] == seg[None, :])
    return jnp.where(allowed[None], scores, far_below)


def attend_forward(scaled, keys, values, seg, rows, count):

    def one_block(index):
        start = index * rows
        query_block = lax.dynamic_slice_in_dim(scaled, start, rows, 0)
        scores = block_scores(query_block, keys, seg, start, rows)
        top = jnp.max(scores, axis=-1, keepdims=True)
        expo = jnp.exp(scores - top)
        denom = jnp.sum(expo, axis=-1, keepdims=True)
        probs = (expo / denom).astype(jnp.bfloat16)
        result = jnp.einsum("hqk,khd->qhd", probs, values, preferred_element_type=jnp.float32)
        return (result, (top + jnp.log(denom))[..., 0])

    return lax.map(one_block, jnp.arange(count, dtype=jnp.int32))


def attend_backward(scaled, keys, values, grad_out, lse, seg, rows, count):
    zeros = jnp.zeros(keys.shape, jnp.float32)

    def one_block(carry, index):
        d_keys, d_values = carry
        start = index * rows
        query_block = lax.dynamic_slice_in_dim(scaled, start, rows, 0)
        grad_block = lax.dynamic_slice_in_dim(grad_out, start, rows, 0)
        scores = block_scores(query_block, keys, seg, start, rows)
        probs = jnp.exp(scores - lse[index][..., None])
        low_probs = probs.astype(jnp.bfloat16)
        d_probs = jnp.einsum("qhd,khd->hqk", grad_block, values, preferred_element_type=jnp.float32)
        d_values = d_values + jnp.einsum(
            "hqk,qhd->khd", low_probs, grad_block, preferred_element_type=jnp.float32
        )
        inner = jnp.sum(d_probs * probs, axis=-1, keepdims=True)
        d_scores = (probs * (d_probs - inner)).astype(jnp.bfloat16)
        d_query = jnp.einsum("hqk,khd->qhd", d_scores, keys, preferred_element_type=jnp.float32)
        d_keys = d_keys + jnp.einsum(
            "hqk,qhd->khd", d_scores, query_block, preferred_element_type=jnp.float32
        )
        return ((d_keys, d_values), d_query)

    (d_keys, d_values), d_query = lax.scan(
        one_block, (zeros, zeros), jnp.arange(count, dtype=jnp.int32)
    )
    return (d_query, d_keys, d_values)


def body(
    tokens,
    segments,
    w_query,
    w_key,
    w_value,
    w_output,
    w_up,
    b_up,
    w_down,
    b_down,
    gain_attn,
    gain_mlp,
    query_scale,
    cotangent,
):
    seg = segments[0]
    length = seg.shape[0]
    rows = min(512, length)
    count = length // rows
    local_heads = w_query.shape[1] // HD
    shape3 = (length, local_heads, HD)
    query_full, key_full, value_full, up_full, output_full, down_full = (
        lax.all_gather(w_query, "dp", axis=0, tiled=True),
        lax.all_gather(w_key, "dp", axis=0, tiled=True),
        lax.all_gather(w_value, "dp", axis=0, tiled=True),
        lax.all_gather(w_up, "dp", axis=0, tiled=True),
        lax.all_gather(w_output, "dp", axis=1, tiled=True),
        lax.all_gather(w_down, "dp", axis=1, tiled=True),
    )
    inputs = tokens.astype(jnp.float32)
    inv_first = row_inverse(inputs)
    normed_first = (inputs * inv_first * gain_attn).astype(jnp.bfloat16)
    first_full = all_rows(normed_first)
    query_raw = jnp.dot(first_full, query_full, preferred_element_type=jnp.float32)
    factor = jax.nn.softplus(query_scale) * (LOG2E / math.sqrt(HD))
    factor_cols = jnp.tile(factor, local_heads)
    scaled = (query_raw * factor_cols).astype(jnp.bfloat16).reshape(shape3)
    keys = (
        jnp.dot(first_full, key_full, preferred_element_type=jnp.float32)
        .astype(jnp.bfloat16)
        .reshape(shape3)
    )
    values = (
        jnp.dot(first_full, value_full, preferred_element_type=jnp.float32)
        .astype(jnp.bfloat16)
        .reshape(shape3)
    )
    attended, lse = attend_forward(scaled, keys, values, seg, rows, count)
    mixed_low = attended.reshape(length, -1).astype(jnp.bfloat16)
    attn = combine(jnp.dot(mixed_low, output_full, preferred_element_type=jnp.float32))
    hidden = inputs + attn
    inv_second = row_inverse(hidden)
    normed_second = (hidden * inv_second * gain_mlp).astype(jnp.bfloat16)
    second_full = all_rows(normed_second)
    preact = jnp.dot(second_full, up_full, preferred_element_type=jnp.float32) + b_up
    active = jax.nn.silu(preact).astype(jnp.bfloat16)
    branch = combine(jnp.dot(active, down_full, preferred_element_type=jnp.float32))
    layer_out = (hidden + branch + b_down).astype(jnp.bfloat16)
    upstream = cotangent.astype(jnp.float32)
    upstream_full = all_rows(cotangent)
    grad_w_down = jnp.einsum("tf,td->fd", active, upstream_full, preferred_element_type=jnp.float32)
    d_active = jnp.einsum("td,fd->tf", upstream_full, down_full, preferred_element_type=jnp.float32)
    sigma = jax.nn.sigmoid(preact)
    d_preact = (d_active * sigma * (1.0 + preact * (1.0 - sigma))).astype(jnp.bfloat16)
    grad_b_up = jnp.sum(d_preact.astype(jnp.float32), axis=0)
    grad_w_up = jnp.einsum("td,tf->df", second_full, d_preact, preferred_element_type=jnp.float32)
    d_second = combine(
        jnp.einsum("tf,df->td", d_preact, up_full, preferred_element_type=jnp.float32)
    )
    grad_gain_mlp = jnp.sum(d_second * hidden * inv_second, axis=0)
    weighted_second = d_second * gain_mlp
    cube_second = inv_second * inv_second * inv_second
    second_dots = jnp.sum(weighted_second * hidden, axis=1, keepdims=True)
    d_hidden = upstream + inv_second * weighted_second - hidden * cube_second / D * second_dots
    d_attn_low = d_hidden.astype(jnp.bfloat16)
    d_attn_full = all_rows(d_attn_low)
    grad_w_output = jnp.einsum(
        "th,td->hd", mixed_low, d_attn_full, preferred_element_type=jnp.float32
    )
    d_mixed = jnp.einsum(
        "td,hd->th", d_attn_full, output_full, preferred_element_type=jnp.float32
    ).astype(jnp.bfloat16)
    d_scaled, d_keys, d_values = attend_backward(
        scaled, keys, values, d_mixed.reshape(shape3), lse, seg, rows, count
    )
    d_scaled_low = d_scaled.reshape(length, -1).astype(jnp.bfloat16).astype(jnp.float32)
    scale_part = jnp.sum((d_scaled_low * query_raw).reshape(shape3), axis=(0, 1))
    d_query = (d_scaled_low * factor_cols).astype(jnp.bfloat16)
    d_keys_low = d_keys.reshape(length, -1).astype(jnp.bfloat16)
    d_values_low = d_values.reshape(length, -1).astype(jnp.bfloat16)
    grad_w_query = jnp.einsum("td,th->dh", first_full, d_query, preferred_element_type=jnp.float32)
    grad_w_key = jnp.einsum("td,th->dh", first_full, d_keys_low, preferred_element_type=jnp.float32)
    grad_w_value = jnp.einsum(
        "td,th->dh", first_full, d_values_low, preferred_element_type=jnp.float32
    )
    d_first_terms = jnp.einsum("th,dh->td", d_query, query_full, preferred_element_type=jnp.float32)
    d_first_terms = d_first_terms + jnp.einsum(
        "th,dh->td", d_keys_low, key_full, preferred_element_type=jnp.float32
    )
    d_first_terms = d_first_terms + jnp.einsum(
        "th,dh->td", d_values_low, value_full, preferred_element_type=jnp.float32
    )
    d_first = combine(d_first_terms)
    grad_gain_attn = jnp.sum(d_first * inputs * inv_first, axis=0)
    weighted_first = d_first * gain_attn
    cube_first = inv_first * inv_first * inv_first
    first_dots = jnp.sum(weighted_first * inputs, axis=1, keepdims=True)
    d_inputs = d_hidden + inv_first * weighted_first - inputs * cube_first / D * first_dots
    tokens_grad = d_inputs.astype(jnp.bfloat16)
    sum_gain_attn, sum_gain_mlp, sum_b_down, scale_total = lax.psum(
        (grad_gain_attn, grad_gain_mlp, jnp.sum(upstream, axis=0), scale_part), ("dp", "mp")
    )
    grad_query_scale = scale_total * (LOG2E / math.sqrt(HD)) * jax.nn.sigmoid(query_scale)
    sum_b_up = lax.psum(grad_b_up, "dp")
    owned_query, owned_key, owned_value, owned_up, owned_output, owned_down = (
        lax.psum_scatter(grad_w_query, "dp", scatter_dimension=0, tiled=True),
        lax.psum_scatter(grad_w_key, "dp", scatter_dimension=0, tiled=True),
        lax.psum_scatter(grad_w_value, "dp", scatter_dimension=0, tiled=True),
        lax.psum_scatter(grad_w_up, "dp", scatter_dimension=0, tiled=True),
        lax.psum_scatter(grad_w_output, "dp", scatter_dimension=1, tiled=True),
        lax.psum_scatter(grad_w_down, "dp", scatter_dimension=1, tiled=True),
    )
    return (
        layer_out,
        tokens_grad,
        owned_query,
        owned_key,
        owned_value,
        owned_output,
        owned_up,
        sum_b_up,
        owned_down,
        sum_b_down,
        sum_gain_attn,
        sum_gain_mlp,
        grad_query_scale,
    )


def solution(mesh):
    return jax.shard_map(
        body,
        mesh=mesh,
        in_specs=(
            P(("dp", "mp"), None),
            P("dp", None),
            P("dp", "mp"),
            P("dp", "mp"),
            P("dp", "mp"),
            P("mp", "dp"),
            P("dp", "mp"),
            P("mp"),
            P("mp", "dp"),
            P(),
            P(),
            P(),
            P(),
            P(("dp", "mp"), None),
        ),
        out_specs=(
            P(("dp", "mp"), None),
            P(("dp", "mp"), None),
            P("dp", "mp"),
            P("dp", "mp"),
            P("dp", "mp"),
            P("mp", "dp"),
            P("dp", "mp"),
            P("mp"),
            P("mp", "dp"),
            P(),
            P(),
            P(),
            P(),
        ),
        check_vma=False,
    )
```

profile of v0, /device:TPU:0, one launch (start us, length us, event | category | flops | bytes accessed | tf_op | source)
XLA Modules:
  0.0 1751.4 jit_solution(3434852759785778891)
XLA Ops:
  13.1 13.3 all_gather.31
  26.4 11.9 all_gather.32
  38.3 10.8 all_gather.33
  49.1 11.5 all_gather.34
  60.5 53.3 %all-gather.5.cloned.1.call-done = bf16[2048,1280]{1,0:T(8,128)(2,1)} async-done(((bf16[512,1280]{1,0:T(8,128)(2,1)}), bf16[2048,1280]{1,0:T(8,128)(2,1)}) %all-gather.5.cloned.1.call-update) | async-done | bytes 5242896 | tf_op jit(solution)/shard_map/all_gather | solution.py:22
  125.5 63.9 %while.27 = (s32[]{:T(128)}, bf16[4,512,4,80]{1,3,2,0:T(8,128)(2,1)}, f32[4,4,512]{2,1,0:T(4,128)S(1)}, s32[4]{0:T(128)S(1)}, s32[2048]{0:T(1024)S(1)}, /*index=...) while((s32[]{:T(128)}, ...), condition=%wide.region_4.5_spmd, body=%wide.region_1.4_spmd.sunk | while | flops 1383070208 | bytes 68700432 | solution.py:52
  199.0 176.5 %reduce-scatter.11.cloned.1.call-done = f32[512,1280]{1,0:T(8,128)} async-done(((f32[2048,1280]{1,0:T(8,128)}), f32[512,1280]{1,0:T(8,128)}) %reduce-scatter.11.cloned.1.call-update) | async-done | bytes 2621456 | tf_op jit(solution)/shard_map/reduce_scatter | solution.py:26
  381.5 11.8 all_gather.36
  393.4 12.3 all_gather.37
  405.6 74.5 %all-gather.7.cloned.1.call-done = bf16[2048,1280]{1,0:T(8,128)(2,1)} async-done(((bf16[512,1280]{1,0:T(8,128)(2,1)}), bf16[2048,1280]{1,0:T(8,128)(2,1)}) %all-gather.7.cloned.1.call-update) | async-done | bytes 5242896 | tf_op jit(solution)/shard_map/all_gather | solution.py:22
  480.1 6.1 convolution_add_fusion
  486.3 91.8 %all-gather.9.cloned.1.call-done = bf16[2048,1280]{1,0:T(8,128)(2,1)} async-done(((bf16[512,1280]{1,0:T(8,128)(2,1)}), bf16[2048,1280]{1,0:T(8,128)(2,1)}) %all-gather.9.cloned.1.call-update) | async-done | bytes 5242896 | tf_op jit(solution)/shard_map/all_gather | solution.py:22
  578.0 6.9 convert_reduce_fusion.1
  591.7 9.0 fusion.51
  600.8 167.4 %reduce-scatter.15.cloned.1.call-done = f32[512,1280]{1,0:T(8,128)} async-done(((f32[2048,1280]{1,0:T(8,128)}), f32[512,1280]{1,0:T(8,128)}) %reduce-scatter.15.cloned.1.call-update) | async-done | bytes 2621456 | tf_op jit(solution)/shard_map/reduce_scatter | solution.py:26
  772.0 177.5 %reduce-scatter.13.cloned.1.call-done = f32[512,1280]{1,0:T(8,128)} async-done(((f32[2048,1280]{1,0:T(8,128)}), f32[512,1280]{1,0:T(8,128)}) %reduce-scatter.13.cloned.1.call-update) | async-done | bytes 2621456 | tf_op jit(solution)/shard_map/reduce_scatter | solution.py:26
  949.5 6.4 fusion.52
  956.0 99.2 %all-gather.11.cloned.1.call-done = bf16[2048,1280]{1,0:T(8,128)(2,1)} async-done(((bf16[512,1280]{1,0:T(8,128)(2,1)}), bf16[2048,1280]{1,0:T(8,128)(2,1)}) %all-gather.11.cloned.1.call-update) | async-done | bytes 5242896 | tf_op jit(solution)/shard_map/all_gather | solution.py:22
  1055.2 5.8 convolution_convert_fusion
  1062.1 214.8 %while.28 = (s32[]{:T(128)}, f32[2048,4,80]{0,2,1:T(8,128)}, f32[2048,4,80]{0,2,1:T(8,128)}, bf16[4,512,4,80]{1,3,2,0:T(8,128)(2,1)}, s32[4]{0:T(128)S(1)}, /*in...) while((s32[]{:T(128)}, f32[2048,4,80]{0,2,1:T(8,128)}, ...), condition=%wide.region_12.13_spmd.clone, body=%wide.region_10.12_spmd.clone.sunk | while | flops 3411540480 | bytes 234564016 | solution.py:78
  1070.1 5.7 copy-done
  1075.8 7.0 fusion.136
  1082.8 12.4 multiply_reduce_fusion.6
  1095.2 12.1 multiply_convert_fusion.10
  1127.9 7.9 fusion.136
  1135.8 12.4 multiply_reduce_fusion.6
  1148.2 12.1 multiply_convert_fusion.10
  1182.0 7.9 fusion.136
  1189.8 12.4 multiply_reduce_fusion.6
  1202.2 12.1 multiply_convert_fusion.10
  1236.0 7.9 fusion.136
  1243.9 12.4 multiply_reduce_fusion.6
  1256.3 12.1 multiply_convert_fusion.10
  1291.3 8.9 add_add_fusion
  1301.5 6.7 fusion.60
  1308.3 7.6 fusion.50
  1315.9 6.7 fusion.59
  1322.8 7.2 fusion.58
  1330.3 6.8 fusion.48
  1337.1 7.1 fusion.57
  1344.3 14.6 psum.35
  1362.0 114.8 %reduce-scatter.17.cloned.1.call-done = f32[512,1280]{1,0:T(8,128)} async-done(((f32[2048,1280]{1,0:T(8,128)}), f32[512,1280]{1,0:T(8,128)}) %reduce-scatter.17.cloned.1.call-update) | async-done | bytes 2621456 | tf_op jit(solution)/shard_map/reduce_scatter | solution.py:26
  1479.3 41.9 %all-reduce = (f32[1280]{0:T(1024)}, f32[1280]{0:T(1024)}, f32[1280]{0:T(1024)}, f32[80]{0:T(128)S(1)}) all-reduce(f32[1280]{0:T(1024)S(1)} %copy-done.34, f32[1280]{0:T(1024)S(1)} %get-tuple-element.171, f32[1280]{0:T(1024)S(1)} %copy-done.33, f32[80]{0:T(128)S(1)} %reduce_sum.116), channel_id=1, replica_groups=mesh['dp'=8,'mp'=4] {'dp','mp'}, use_global_device_ids=true, to_apply=%region_24.25 | all-reduce | flops 3920 | bytes 31360 | tf_op jit(solution)/shard_map/psum | solution.py:194
  1526.1 40.8 %reduce-scatter.29.cloned.1.call-done = f32[320,160]{0,1:T(8,128)} async-done(((f32[320,1280]{0,1:T(8,128)}), f32[320,160]{0,1:T(8,128)}) %reduce-scatter.29.cloned.1.call-update) | async-done | bytes 204816 | tf_op jit(solution)/shard_map/reduce_scatter | solution.py:205
  1566.9 44.3 %reduce-scatter.25.cloned.1.call-done = f32[320,160]{0,1:T(8,128)} async-done(((f32[320,1280]{0,1:T(8,128)}), f32[320,160]{0,1:T(8,128)}) %reduce-scatter.25.cloned.1.call-update) | async-done | bytes 204816 | tf_op jit(solution)/shard_map/reduce_scatter | solution.py:204
  1611.2 44.5 %reduce-scatter.23.cloned.1.call-done = f32[160,320]{1,0:T(8,128)} async-done(((f32[1280,320]{1,0:T(8,128)}), f32[160,320]{1,0:T(8,128)}) %reduce-scatter.23.cloned.1.call-update) | async-done | bytes 204816 | tf_op jit(solution)/shard_map/reduce_scatter | solution.py:202
  1655.8 44.3 %reduce-scatter.19.cloned.1.call-done = f32[160,320]{1,0:T(8,128)} async-done(((f32[1280,320]{1,0:T(8,128)}), f32[160,320]{1,0:T(8,128)}) %reduce-scatter.19.cloned.1.call-update) | async-done | bytes 204816 | tf_op jit(solution)/shard_map/reduce_scatter | solution.py:200
  1700.1 44.5 %reduce-scatter.21.cloned.1.call-done = f32[160,320]{1,0:T(8,128)} async-done(((f32[1280,320]{1,0:T(8,128)}), f32[160,320]{1,0:T(8,128)}) %reduce-scatter.21.cloned.1.call-update) | async-done | bytes 204816 | tf_op jit(solution)/shard_map/reduce_scatter | solution.py:201
  (264 shorter events, 201.7 us)
Async XLA Ops:
  7.2 5.8 copy-start.44
  7.2 5.9 copy-start.25
  7.2 106.6 %all-gather.5.cloned.1.call-start = ((), (), s32[]{:S(2)}) async-start(), calls=%async_computation.10 | async-start | bytes 6553600 | tf_op jit(solution)/shard_map/all_gather | solution.py:22
  8.9 17.5 %copy-start.26 = (bf16[160,320]{1,0:T(8,128)(2,1)S(1)}, bf16[160,320]{1,0:T(8,128)(2,1)}, u32[]{:S(2)}) copy-start(bf16[160,320]{1,0:T(8,128)(2,1)} %param.21) | copy-start | bytes 307204
  10.1 28.2 %copy-start.27 = (bf16[160,320]{1,0:T(8,128)(2,1)S(1)}, bf16[160,320]{1,0:T(8,128)(2,1)}, u32[]{:S(2)}) copy-start(bf16[160,320]{1,0:T(8,128)(2,1)} %param.22) | copy-start | bytes 307204
  12.9 36.2 %copy-start.28 = (bf16[320,160]{0,1:T(8,128)(2,1)S(1)}, bf16[320,160]{0,1:T(8,128)(2,1)}, u32[]{:S(2)}) copy-start(bf16[320,160]{0,1:T(8,128)(2,1)} %param.23) | copy-start | bytes 307204
  12.9 362.6 %reduce-scatter.11.cloned.1.call-start = ((), (), s32[]{:S(2)}) async-start(), calls=%async_computation.11 | async-start | bytes 13107200 | tf_op jit(solution)/shard_map/reduce_scatter | solution.py:26
  13.1 107.3 %copy-start.37 = (f32[320]{0:T(512)}, f32[320]{0:T(512)S(1)}, u32[]{:S(2)}) copy-start(f32[320]{0:T(512)S(1)} %mul.216) | copy-start | bytes 3844
  49.1 64.8 %copy-start.15 = (bf16[1280,320]{1,0:T(8,128)(2,1)}, bf16[1280,320]{1,0:T(8,128)(2,1)S(1)}, u32[]{:S(2)}) copy-start(bf16[1280,320]{1,0:T(8,128)(2,1)S(1)} %all_gather.33) | copy-start | bytes 2457604
  199.0 180.5 %copy-start.31 = (f32[1280]{0:T(1024)S(1)}, f32[1280]{0:T(1024)}, u32[]{:S(2)}) copy-start(f32[1280]{0:T(1024)} %param.29) | copy-start | bytes 15364
  199.0 281.2 %all-gather.7.cloned.1.call-start = ((), (), s32[]{:S(2)}) async-start(), calls=%async_computation.12 | async-start | bytes 6553600 | tf_op jit(solution)/shard_map/all_gather | solution.py:22
  380.9 12.5 copy-start.30
  380.9 99.3 %copy-start.43 = (f32[320]{0:T(512)S(1)}, f32[320]{0:T(512)}, u32[]{:S(2)}) copy-start(f32[320]{0:T(512)} %param.25) | copy-start | bytes 3844
  380.9 197.1 %all-gather.9.cloned.1.call-start = ((), (), s32[]{:S(2)}) async-start(), calls=%async_computation.14 | async-start | bytes 6553600 | tf_op jit(solution)/shard_map/all_gather | solution.py:22
  381.5 386.7 %reduce-scatter.15.cloned.1.call-start = ((), (), s32[]{:S(2)}) async-start(), calls=%async_computation.15 | async-start | bytes 13107200 | tf_op jit(solution)/shard_map/reduce_scatter | solution.py:26
  578.0 8.0 copy-start.19
  591.7 357.8 %reduce-scatter.13.cloned.1.call-start = ((), (), s32[]{:S(2)}) async-start(), calls=%async_computation.13 | async-start | bytes 13107200 | tf_op jit(solution)/shard_map/reduce_scatter | solution.py:26
  600.7 348.8 %copy-start.39 = (f32[1280]{0:T(1024)S(1)}, f32[1280]{0:T(1024)}, u32[]{:S(2)}) copy-start(f32[1280]{0:T(1024)} %param.27) | copy-start | bytes 15364
  600.7 454.4 %all-gather.11.cloned.1.call-start = ((), (), s32[]{:S(2)}) async-start(), calls=%async_computation.16 | async-start | bytes 6553600 | tf_op jit(solution)/shard_map/all_gather | solution.py:22
  955.9 520.8 %reduce-scatter.17.cloned.1.call-start = ((), (), s32[]{:S(2)}) async-start(), calls=%async_computation.17 | async-start | bytes 13107200 | tf_op jit(solution)/shard_map/reduce_scatter | solution.py:26
  1070.0 5.7 copy-start
  1095.2 12.1 copy-start.13
  1122.2 5.7 copy-start
  1148.2 12.1 copy-start.13
  1163.0 5.5 copy-start.14
  1163.0 5.5 copy-start.4
  1176.2 5.7 copy-start
  1202.2 12.1 copy-start.13
  1217.0 5.5 copy-start.14
  1230.3 5.7 copy-start
  1256.3 12.1 copy-start.13
  1271.0 5.5 copy-start.14
  1300.2 225.9 %reduce-scatter.27.cloned.1.call-start = ((), (), s32[]{:S(2)}) async-start(), calls=%async_computation.22 | async-start | bytes 2211840 | tf_op jit(solution)/shard_map/reduce_scatter | solution.py:203
  1308.2 7.7 copy-start.9
  1308.2 258.7 %reduce-scatter.29.cloned.1.call-start = ((), (), s32[]{:S(2)}) async-start(), calls=%async_computation.23 | async-start | bytes 2211840 | tf_op jit(solution)/shard_map/reduce_scatter | solution.py:205
  1315.9 295.4 %reduce-scatter.25.cloned.1.call-start = ((), (), s32[]{:S(2)}) async-start(), calls=%async_computation.21 | async-start | bytes 2211840 | tf_op jit(solution)/shard_map/reduce_scatter | solution.py:204
  1322.7 7.6 copy-start.7
  1322.7 333.0 %reduce-scatter.23.cloned.1.call-start = ((), (), s32[]{:S(2)}) async-start(), calls=%async_computation.20 | async-start | bytes 2211840 | tf_op jit(solution)/shard_map/reduce_scatter | solution.py:202
  1330.0 370.1 %reduce-scatter.19.cloned.1.call-start = ((), (), s32[]{:S(2)}) async-start(), calls=%async_computation.18 | async-start | bytes 2211840 | tf_op jit(solution)/shard_map/reduce_scatter | solution.py:200
  1337.1 7.2 copy-start.41
  1337.1 407.5 %reduce-scatter.21.cloned.1.call-start = ((), (), s32[]{:S(2)}) async-start(), calls=%async_computation.19 | async-start | bytes 2211840 | tf_op jit(solution)/shard_map/reduce_scatter | solution.py:201
  1358.9 117.9 %copy-start.5 = (bf16[512,1280]{1,0:T(8,128)(2,1)S(1)}, bf16[512,1280]{1,0:T(8,128)(2,1)}, u32[]{:S(2)}) copy-start(bf16[512,1280]{1,0:T(8,128)(2,1)} %param.18) | copy-start | bytes 3932164
  1358.9 117.9 %copy-start.32 = (f32[1280]{0:T(1024)S(1)}, f32[1280]{0:T(1024)}, u32[]{:S(2)}) copy-start(f32[1280]{0:T(1024)} %param.28) | copy-start | bytes 15364
  1358.9 117.9 %copy-start.36 = (f32[512]{0:T(512)S(1)}, f32[512]{0:T(512)}, u32[]{:S(2)}) copy-start(f32[512]{0:T(512)} %copy-done.35) | copy-start | bytes 6148
  1361.8 117.5 %copy-start.33 = (f32[1280]{0:T(1024)S(1)}, f32[1280]{0:T(1024)}, u32[]{:S(2)}) copy-start(f32[1280]{0:T(1024)} %get-tuple-element.169) | copy-start | bytes 15364
  1361.8 117.5 %copy-start.34 = (f32[1280]{0:T(1024)S(1)}, f32[1280]{0:T(1024)}, u32[]{:S(2)}) copy-start(f32[1280]{0:T(1024)} %get-tuple-element.228) | copy-start | bytes 15364
  1361.8 159.4 %copy-start.45 = (f32[80]{0:T(128)S(1)}, f32[80]{0:T(128)}, u32[]{:S(2)}) copy-start(f32[80]{0:T(128)} %param.30) | copy-start | bytes 964
  1361.9 159.9 %copy-start.40 = (f32[512]{0:T(512)S(1)}, f32[512]{0:T(512)}, u32[]{:S(2)}) copy-start(f32[512]{0:T(512)} %get-tuple-element.229) | copy-start | bytes 6148
  (33 other events, 101.3 us)
Sparse Core Ops, SparseCore 0:
  13.0 100.7 all-gather.4
  199.1 176.3 reduce-scatter.10
  381.0 99.0 all-gather.6
  481.6 96.4 all-gather.8
  591.8 176.3 reduce-scatter.14
  770.4 179.0 reduce-scatter.12
  956.0 99.0 all-gather.10
  1300.3 176.3 reduce-scatter.16
  1480.7 41.7 reduce-scatter.26
  1526.8 40.0 reduce-scatter.28
  1570.9 40.2 reduce-scatter.24
  1615.5 40.2 reduce-scatter.22
  1659.7 40.2 reduce-scatter.18
  1704.3 40.2 reduce-scatter.20
where the time goes:
time: 1760 us; the launch traced here: 1750 us
  waiting for transfers between devices  1170 us (66%)
  matrix products  266 us (15%)
  blocking collectives  128 us (7%)
  other arithmetic  106 us (6%)
  local copies, waits for them, and re-layouts  47.6 us (3%)
    reduce_scatter x4, waiting for transfers between devices, combine(): return lax.psum_scatter(values, 'mp', scatter_dimension=0, tiled=True)  636 us
    all_gather x4, waiting for transfers between devices, all_rows(): return lax.all_gather(values, 'mp', axis=0, tiled=True)  319 us
    dot_general x4, matrix products, one_block(): jnp.einsum('qhd,khd->hqk', grad_block, values, preferred_element_type=jnp...  49.7 us
    convert_element_type x4, other arithmetic, one_block(): d_scores = (probs * (d_probs - inner)).astype(jnp.bfloat16)  48.3 us
    reduce_scatter x1, waiting for transfers between devices, body(): lax.psum_scatter(grad_w_value, 'dp', scatter_dimension=0, tiled=True)  44.5 us
    reduce_scatter x1, waiting for transfers between devices, body(): lax.psum_scatter(grad_w_key, 'dp', scatter_dimension=0, tiled=True)  44.5 us
    reduce_scatter x1, waiting for transfers between devices, body(): lax.psum_scatter(grad_w_output, 'dp', scatter_dimension=1, tiled=True)  44.3 us
    reduce_scatter x1, waiting for transfers between devices, body(): lax.psum_scatter(grad_w_query, 'dp', scatter_dimension=0, tiled=True)  44.3 us
  transfers between devices with their start and end apart: 14, of which 13 were waited for; matrix products, arithmetic and copies ran while one was open for 4% of the time, Pallas kernels for 0%

commit v1 on v0

v1 whole, which is shorter than its diff:
```python
import functools
import math

import jax
import jax.numpy as jnp
from jax import lax
from jax.experimental import pallas as pl
from jax.experimental.pallas import tpu as pltpu
from jax.sharding import PartitionSpec as P

HD = 80
LANES = 128
EPSILON = 1e-06
LOG2E = 1.442695
DOC_MAX = 1024
GROUP = 8
FAR = -1e30
F32 = jnp.float32
BF16 = jnp.bfloat16


def dot(a, b, ca, cb):
    return lax.dot_general(a, b, (((ca,), (cb,)), ((), ())), preferred_element_type=F32)


def row_inverse(values):
    return lax.rsqrt(jnp.mean(values * values, axis=1, keepdims=True) + EPSILON)


def split_heads(src, dst, rows):
    def step(index, carry):
        at = pl.ds(pl.multiple_of(index * rows, rows), rows)
        block = src[at, :]
        pad = jnp.zeros((rows, LANES - HD), block.dtype)
        for h in range(GROUP):
            dst[h, at, :] = jnp.concatenate([block[:, HD * h : HD * (h + 1)], pad], axis=1)
        return carry

    lax.fori_loop(0, src.shape[0] // rows, step, 0)


def join_heads(src, dst, rows):
    def step(index, carry):
        at = pl.ds(pl.multiple_of(index * rows, rows), rows)
        dst[at, :] = jnp.concatenate([src[h, at, :HD] for h in range(GROUP)], axis=1)
        return carry

    lax.fori_loop(0, dst.shape[0] // rows, step, 0)


def fill_bias(low_ref, seg_query, seg_key, bias, block, own):
    count = seg_query.shape[1] // block
    for qb in range(count):
        row = seg_query[:, qb * block : (qb + 1) * block]
        pos_query = own + qb * block + lax.broadcasted_iota(jnp.int32, (block, block), 1)
        sub = lax.broadcasted_iota(jnp.int32, (block, block), 0)

        def step(kb, carry):
            at = pl.ds(pl.multiple_of(kb * block, block), block)
            allowed = (seg_key[at, :] == row) & (sub + kb * block <= pos_query)
            bias[qb, at, :] = jnp.where(allowed, 0.0, FAR)
            return carry

        lax.fori_loop(low_ref[qb], own // block + qb + 1, step, 0)


def forward_kernel(
    block, own, low_ref, q_ref, k_ref, v_ref, seg_query, seg_key, o_ref, lse_ref,
    qh, kh, vt, oh, bias, scores,
):
    count = q_ref.shape[0] // block

    @pl.when(pl.program_id(0) == 0)
    def _():
        fill_bias(low_ref, seg_query, seg_key, bias, block, own)

    split_heads(q_ref, qh, block)
    split_heads(k_ref, kh, block)

    def turn(kb, carry):
        at = pl.ds(pl.multiple_of(kb * block, block), block)
        tile = v_ref[at, :]
        pad = jnp.zeros((block, LANES - HD), tile.dtype)
        for h in range(GROUP):
            one = jnp.concatenate([tile[:, HD * h : HD * (h + 1)], pad], axis=1)
            vt[h, kb] = one.T
        return carry

    lax.fori_loop(0, k_ref.shape[0] // block, turn, 0)
    for qb in range(count):
        low, high = low_ref[qb], own // block + qb + 1
        span = pl.ds(qb * block, block)

        def head(h, carry):
            query = qh[h, span, :]

            def first(kb, top):
                at = pl.ds(pl.multiple_of(kb * block, block), block)
                s = dot(kh[h, at, :], query, 1, 1) + bias[qb, at, :]
                scores[at, :] = s
                return jnp.maximum(top, jnp.max(s.reshape(block // 8, 8, block), axis=0))

            top = lax.fori_loop(low, high, first, jnp.full((8, block), FAR, F32))
            top = jnp.max(top, axis=0, keepdims=True)

            def second(kb, state):
                total, acc = state
                at = pl.ds(pl.multiple_of(kb * block, block), block)
                p = jnp.exp(scores[at, :] - top)
                total = total + jnp.sum(p.reshape(block // 8, 8, block), axis=0)
                acc = acc + dot(vt[h, kb], p.astype(BF16), 1, 0)
                return total, acc

            total, acc = lax.fori_loop(
                low, high, second, (jnp.zeros((8, block), F32), jnp.zeros((LANES, block), F32))
            )
            total = jnp.sum(total, axis=0, keepdims=True)
            oh[h, span, :] = (acc / total).T.astype(BF16)
            lse_ref[pl.ds(h, 1), span] = top + jnp.log(total)
            return carry

        lax.fori_loop(0, GROUP, head, 0)
    join_heads(oh, o_ref, block)


def backward_kernel(
    block, own, low_ref, q_ref, k_ref, v_ref, g_ref, lse_ref, delta_ref, seg_query, seg_key,
    dq_ref, dk_ref, dv_ref, qh, gh, kh, vh, kt, dqh, dkh, dvh, dk_acc, dv_acc, bias,
):
    count = q_ref.shape[0] // block
    blocks = k_ref.shape[0] // block

    @pl.when(pl.program_id(0) == 0)
    def _():
        fill_bias(low_ref, seg_query, seg_key, bias, block, own)

    split_heads(q_ref, qh, block)
    split_heads(g_ref, gh, block)
    split_heads(k_ref, kh, block)
    split_heads(v_ref, vh, block)

    def head(h, carry):
        def turn(kb, inner):
            at = pl.ds(pl.multiple_of(kb * block, block), block)
            kt[kb] = kh[h, at, :].T
            dk_acc[at, :] = jnp.zeros((block, LANES), F32)
            dv_acc[at, :] = jnp.zeros((block, LANES), F32)
            return inner

        lax.fori_loop(0, blocks, turn, 0)
        for qb in range(count):
            span = pl.ds(qb * block, block)
            query, grad = qh[h, span, :], gh[h, span, :]
            lse, delta = lse_ref[pl.ds(h, 1), span], delta_ref[pl.ds(h, 1), span]

            def step(kb, acc):
                at = pl.ds(pl.multiple_of(kb * block, block), block)
                s = dot(kh[h, at, :], query, 1, 1) + bias[qb, at, :]
                p = jnp.exp(s - lse)
                dp = dot(vh[h, at, :], grad, 1, 1)
                ds = (p * (dp - delta)).astype(BF16)
                dv_acc[at, :] += dot(p.astype(BF16), grad, 1, 0)
                dk_acc[at, :] += dot(ds, query, 1, 0)
                return acc + dot(kt[kb], ds, 1, 0)

            acc = lax.fori_loop(
                low_ref[qb], own // block + qb + 1, step, jnp.zeros((LANES, block), F32)
            )
            dqh[h, span, :] = acc.T.astype(BF16)

        def keep(kb, inner):
            at = pl.ds(pl.multiple_of(kb * block, block), block)
            dkh[h, at, :] = dk_acc[at, :].astype(BF16)
            dvh[h, at, :] = dv_acc[at, :].astype(BF16)
            return inner

        lax.fori_loop(0, blocks, keep, 0)
        return carry

    lax.fori_loop(0, GROUP, head, 0)
    join_heads(dqh, dq_ref, block)
    join_heads(dkh, dk_ref, block)
    join_heads(dvh, dv_ref, block)


def attention_specs(rows, width, features):
    cols = GROUP * HD
    by_group = lambda n: pl.BlockSpec((n, cols), lambda g, low: (0, g))
    stats = pl.BlockSpec((GROUP, rows), lambda g, low: (g, 0))
    seg_q = pl.BlockSpec((1, rows), lambda g, low: (0, 0))
    seg_k = pl.BlockSpec((width, 1), lambda g, low: (0, 0))
    return by_group, stats, seg_q, seg_k


def attend_forward(low, q, k, v, seg_query, seg_key, block):
    rows, features = q.shape
    width = k.shape[0]
    by_group, stats, seg_q, seg_k = attention_specs(rows, width, features)
    heads = features // HD
    return pl.pallas_call(
        functools.partial(forward_kernel, block, width - rows),
        grid_spec=pltpu.PrefetchScalarGridSpec(
            num_scalar_prefetch=1,
            grid=(heads // GROUP,),
            in_specs=[by_group(rows), by_group(width), by_group(width), seg_q, seg_k],
            out_specs=[by_group(rows), stats],
            scratch_shapes=[
                pltpu.VMEM((GROUP, rows, LANES), BF16),
                pltpu.VMEM((GROUP, width, LANES), BF16),
                pltpu.VMEM((GROUP, width // block, LANES, block), BF16),
                pltpu.VMEM((GROUP, rows, LANES), BF16),
                pltpu.VMEM((rows // block, width, block), F32),
                pltpu.VMEM((width, block), F32),
            ],
        ),
        out_shape=[
            jax.ShapeDtypeStruct((rows, features), BF16),
            jax.ShapeDtypeStruct((heads, rows), F32),
        ],
        compiler_params=pltpu.CompilerParams(vmem_limit_bytes=48 << 20),
        cost_estimate=pl.CostEstimate(
            flops=4 * rows * width * features, bytes_accessed=4 * (rows + width) * features,
            transcendentals=rows * width * heads,
        ),
        name="attend_forward",
    )(low, q, k, v, seg_query, seg_key)


def attend_backward(low, q, k, v, grad, lse, delta, seg_query, seg_key, block):
    rows, features = q.shape
    width = k.shape[0]
    by_group, stats, seg_q, seg_k = attention_specs(rows, width, features)
    heads = features // HD
    return pl.pallas_call(
        functools.partial(backward_kernel, block, width - rows),
        grid_spec=pltpu.PrefetchScalarGridSpec(
            num_scalar_prefetch=1,
            grid=(heads // GROUP,),
            in_specs=[
                by_group(rows), by_group(width), by_group(width), by_group(rows),
                stats, stats, seg_q, seg_k,
            ],
            out_specs=[by_group(rows), by_group(width), by_group(width)],
            scratch_shapes=[
                pltpu.VMEM((GROUP, rows, LANES), BF16),
                pltpu.VMEM((GROUP, rows, LANES), BF16),
                pltpu.VMEM((GROUP, width, LANES), BF16),
                pltpu.VMEM((GROUP, width, LANES), BF16),
                pltpu.VMEM((width // block, LANES, block), BF16),
                pltpu.VMEM((GROUP, rows, LANES), BF16),
                pltpu.VMEM((GROUP, width, LANES), BF16),
                pltpu.VMEM((GROUP, width, LANES), BF16),
                pltpu.VMEM((width, LANES), F32),
                pltpu.VMEM((width, LANES), F32),
                pltpu.VMEM((rows // block, width, block), F32),
            ],
        ),
        out_shape=[
            jax.ShapeDtypeStruct((rows, features), BF16),
            jax.ShapeDtypeStruct((width, features), BF16),
            jax.ShapeDtypeStruct((width, features), BF16),
        ],
        compiler_params=pltpu.CompilerParams(vmem_limit_bytes=56 << 20),
        cost_estimate=pl.CostEstimate(
            flops=10 * rows * width * features, bytes_accessed=6 * (rows + width) * features,
            transcendentals=rows * width * heads,
        ),
        name="attend_backward",
    )(low, q, k, v, grad, lse, delta, seg_query, seg_key)


def gather_weight(block, row_axis, col_axis):
    wide = lax.all_gather(block, "mp", axis=1 if col_axis == "mp" else 0, tiled=True)
    return lax.all_gather(wide, "dp", axis=1 if col_axis == "dp" else 0, tiled=True)


def scatter_grad(grad, row_axis, col_axis):
    low = grad.astype(BF16)
    mine = lax.psum_scatter(low, "dp", scatter_dimension=1 if col_axis == "dp" else 0, tiled=True)
    mine = lax.psum_scatter(mine, "mp", scatter_dimension=1 if col_axis == "mp" else 0, tiled=True)
    return mine.astype(F32)


def body(
    tokens, segments, w_query, w_key, w_value, w_output, w_up, b_up, w_down, b_down,
    gain_attn, gain_mlp, query_scale, cotangent,
):
    stages = lax.axis_size("mp")
    z = lax.axis_index("mp")
    seg = segments[0]
    rows, features = tokens.shape
    back = min(stages - 1, -(-(DOC_MAX - 1) // rows))
    own = back * rows
    block = min(256, rows)
    up = [(i, i + 1) for i in range(stages - 1)]
    down = [(i + 1, i) for i in range(stages - 1)]

    wq, wk, wv, wu = (
        gather_weight(w, "dp", "mp") for w in (w_query, w_key, w_value, w_up)
    )
    wo, wd = (gather_weight(w, "mp", "dp") for w in (w_output, w_down))
    b_full = lax.all_gather(b_up, "mp", axis=0, tiled=True)

    inputs = tokens.astype(F32)
    inv_first = row_inverse(inputs)
    normed = (inputs * inv_first * gain_attn).astype(BF16)
    window = [normed]
    for _ in range(back):
        window.append(lax.ppermute(window[-1], "mp", up))
    first = jnp.concatenate(window[::-1], axis=0)

    seg_wide = jnp.concatenate([jnp.full((own,), -1, jnp.int32), seg])
    seg_window = lax.dynamic_slice_in_dim(seg_wide, z * rows, own + rows, 0)
    seg_query = seg_window[own:]
    heads_of_block = seg_query[::block]
    low = jnp.sum(seg_window[None, :] < heads_of_block[:, None], axis=1, dtype=jnp.int32) // block
    seg_query, seg_key = seg_query[None, :], seg_window[:, None]

    heads = features // HD
    factor = jax.nn.softplus(query_scale) * (LOG2E / math.sqrt(HD))
    factor_cols = jnp.tile(factor, heads)
    query_raw = jnp.dot(normed, wq, preferred_element_type=F32)
    scaled = (query_raw * factor_cols).astype(BF16)
    keys = jnp.dot(first, wk, preferred_element_type=F32).astype(BF16)
    values = jnp.dot(first, wv, preferred_element_type=F32).astype(BF16)
    mixed, lse = attend_forward(low, scaled, keys, values, seg_query, seg_key, block)

    hidden = inputs + jnp.dot(mixed, wo, preferred_element_type=F32)
    inv_second = row_inverse(hidden)
    second = (hidden * inv_second * gain_mlp).astype(BF16)
    preact = jnp.dot(second, wu, preferred_element_type=F32) + b_full
    active = jax.nn.silu(preact).astype(BF16)
    layer_out = (hidden + jnp.dot(active, wd, preferred_element_type=F32) + b_down).astype(BF16)

    upstream = cotangent.astype(F32)
    sigma = jax.nn.sigmoid(preact)
    d_active = dot(cotangent, wd, 1, 1)
    d_preact = (d_active * sigma * (1.0 + preact * (1.0 - sigma))).astype(BF16)
    d_second = dot(d_preact, wu, 1, 1)
    weighted = d_second * gain_mlp
    dots = jnp.sum(weighted * hidden, axis=1, keepdims=True)
    cube = inv_second * inv_second * inv_second
    d_hidden = upstream + inv_second * weighted - hidden * cube / features * dots
    d_attn = d_hidden.astype(BF16)
    d_mixed = dot(d_attn, wo, 1, 1).astype(BF16)

    owner = (jnp.arange(features)[None, :] // HD == jnp.arange(heads)[:, None]).astype(F32)
    delta = lax.dot_general(
        owner, d_mixed.astype(F32) * mixed.astype(F32), (((1,), (1,)), ((), ())),
        precision=lax.Precision.HIGHEST, preferred_element_type=F32,
    )
    d_scaled, d_keys, d_values = attend_backward(
        low, scaled, keys, values, d_mixed, lse, delta, seg_query, seg_key, block
    )
    d_scaled_wide = d_scaled.astype(F32)
    d_query = (d_scaled_wide * factor_cols).astype(BF16)
    scale_part = jnp.sum(jnp.sum(d_scaled_wide * query_raw, axis=0).reshape(heads, HD), axis=0)

    part = None
    for c in range(back + 1):
        at = slice(c * rows, (c + 1) * rows)
        term = dot(d_keys[at], wk, 1, 1) + dot(d_values[at], wv, 1, 1)
        if c == back:
            term = term + dot(d_query, wq, 1, 1)
        if part is not None:
            term = term + part
        if c < back:
            part = lax.ppermute(term.astype(BF16), "mp", down).astype(F32)
    d_first = term

    weighted_first = d_first * gain_attn
    cube_first = inv_first * inv_first * inv_first
    first_dots = jnp.sum(weighted_first * inputs, axis=1, keepdims=True)
    tokens_grad = (
        d_hidden + inv_first * weighted_first - inputs * cube_first / features * first_dots
    ).astype(BF16)

    grad_gain_attn = jnp.sum(d_first * inputs * inv_first, axis=0)
    grad_gain_mlp = jnp.sum(d_second * hidden * inv_second, axis=0)
    grad_b_up = jnp.sum(d_preact.astype(F32), axis=0)
    sums = jnp.concatenate(
        [grad_gain_mlp, jnp.sum(upstream, axis=0), grad_b_up, grad_gain_attn, scale_part]
    )
    sums = lax.psum(sums, ("dp", "mp"))
    sum_gain_mlp, sum_b_down, sum_b_up, sum_gain_attn, scale_total = jnp.split(
        sums, [features, 2 * features, 3 * features, 4 * features]
    )
    mine = b_up.shape[0]
    sum_b_up = lax.dynamic_slice_in_dim(sum_b_up, z * mine, mine, 0)
    grad_query_scale = scale_total * (LOG2E / math.sqrt(HD)) * jax.nn.sigmoid(query_scale)

    grads = (
        scatter_grad(dot(normed, d_query, 0, 0), "dp", "mp"),
        scatter_grad(dot(first, d_keys, 0, 0), "dp", "mp"),
        scatter_grad(dot(first, d_values, 0, 0), "dp", "mp"),
        scatter_grad(dot(mixed, d_attn, 0, 0), "mp", "dp"),
        scatter_grad(dot(second, d_preact, 0, 0), "dp", "mp"),
        scatter_grad(dot(active, cotangent, 0, 0), "mp", "dp"),
    )
    return (
        layer_out, tokens_grad, grads[0], grads[1], grads[2], grads[3], grads[4], sum_b_up,
        grads[5], sum_b_down, sum_gain_attn, sum_gain_mlp, grad_query_scale,
    )


def solution(mesh):
    tokens, rows_dp, rows_mp = P(("dp", "mp"), None), P("dp", "mp"), P("mp", "dp")
    return jax.shard_map(
        body,
        mesh=mesh,
        in_specs=(
            tokens, P("dp", None), rows_dp, rows_dp, rows_dp, rows_mp, rows_dp, P("mp"), rows_mp,
            P(), P(), P(), P(), tokens,
        ),
        out_specs=(
            tokens, tokens, rows_dp, rows_dp, rows_dp, rows_mp, rows_dp, P("mp"), rows_mp,
            P(), P(), P(), P(),
        ),
        check_vma=False,
    )
```

time: 1760 us -> 734 us (0.42)
  waiting for transfers between devices: 1170 us -> 259 us
  matrix products: 266 us -> 131 us
  other arithmetic: 106 us -> 11.8 us
  Pallas kernels: 0 us -> 92.2 us
  blocking collectives: 128 us -> 171 us
    reduce_scatter x10 -> x6, waiting for transfers between devices: 855 us -> 114 us  [scatter_grad(): lax.psum_scatter(low, 'dp', scatter_dimension=1 if col_axis == 'dp' else...]
    all_gather x4 -> x6, waiting for transfers between devices: 319 us -> 0.03 us  [gather_weight(): lax.all_gather(wide, 'dp', axis=1 if col_axis == 'dp' else 0, tiled=True)]
    dot_general x46 -> x23, matrix products: 266 us -> 131 us  [the longest x16 84 us: dot(): lax.dot_general(a, b, (((ca,), (cb,)), ((), ())), preferred_element_type=...]
    unnamed x14 -> x24, waiting for transfers between devices: 0.73 us -> 125 us
    pallas_call x0 -> x2, Pallas kernels: none -> 92.2 us  [the longest x1 52.7 us: attend_backward(): pl.pallas_call(functools.partial(backward_kernel, block, width - rows), g...]
    convert_element_type x10 -> x8, other arithmetic: 67.3 us -> 9.45 us  [the longest x1 4.8 us: body(): tokens_grad = (d_hidden + inv_first * weighted_first - inputs * cube_firs...]
    all_gather x6, blocking collectives: 71.5 us -> 112 us  [gather_weight(): lax.all_gather(block, 'mp', axis=1 if col_axis == 'mp' else 0, tiled=True)]
    while x56 -> x0, local copies, waits for them, and re-layouts: 27.1 us -> none
  transfers between devices with their start and end apart: 14 -> 22, of which waited for: 13 -> 12; matrix products, arithmetic and copies ran while one was open for 4% -> 22% of each run, Pallas kernels for 0% -> 13%
where the time goes in v1:
time: 734 us; the launch traced here: 728 us
  waiting for transfers between devices  259 us (35%)
  blocking collectives  171 us (23%)
  matrix products  131 us (18%)
  Pallas kernels  92.2 us (13%)
  local copies, waits for them, and re-layouts  35.3 us (5%)
  between operations  15.8 us (2%)
  starting transfers between devices  12.7 us (2%)
  other arithmetic  11.8 us (2%)
    unnamed x24, waiting for transfers between devices  125 us
    reduce_scatter x6, waiting for transfers between devices, scatter_grad(): lax.psum_scatter(low, 'dp', scatter_dimension=1 if col_axis == 'dp' else...  114 us
    all_gather x6, blocking collectives, gather_weight(): lax.all_gather(block, 'mp', axis=1 if col_axis == 'mp' else 0, tiled=True)  112 us
    dot_general x16, matrix products, dot(): lax.dot_general(a, b, (((ca,), (cb,)), ((), ())), preferred_element_type=...  84 us
    pallas_call x1, Pallas kernels, attend_backward(): pl.pallas_call(functools.partial(backward_kernel, block, width - rows), g...  52.7 us
    psum x1, blocking collectives, body(): sums = lax.psum(sums, ('dp', 'mp'))  39.6 us
    pallas_call x1, Pallas kernels, attend_forward(): pl.pallas_call(functools.partial(forward_kernel, block, width - rows), gr...  39.5 us
    unnamed x99, local copies, waits for them, and re-layouts  31.8 us
  transfers between devices with their start and end apart: 22, of which 12 were waited for; matrix products, arithmetic and copies ran while one was open for 22% of the time, Pallas kernels for 13%

profile of v1, /device:TPU:0, one launch (start us, length us, event | category | flops | bytes accessed | tf_op | source)
XLA Modules:
  0.0 728.3 jit_solution(1843978978469213722)
XLA Ops:
  7.2 17.2 %all-gather = bf16[4,320,160]{1,2,0:T(8,128)(2,1)S(1)} all-gather(bf16[1,320,160]{1,2,0:T(8,128)(2,1)} %bitcast.83), channel_id=1, replica_groups=mesh['dp'=8,'mp'=4] {'mp'}, dimensions={0}, use_global_device_ids=true | all-gather | bytes 512000 | tf_op jit(solution)/shard_map/all_gather | solution.py:273
  25.9 15.9 %all-gather.2 = bf16[4,320,160]{1,2,0:T(8,128)(2,1)S(1)} all-gather(bf16[1,320,160]{1,2,0:T(8,128)(2,1)S(1)} %bitcast.84), channel_id=1, replica_groups=mesh['dp'=8,'mp'=4] {'mp'}, dimensions={0}, use_global_device_ids=true | all-gather | bytes 512000 | tf_op jit(solution)/shard_map/all_gather | solution.py:273
  43.3 15.4 %all-gather.1 = bf16[4,320,160]{1,2,0:T(8,128)(2,1)S(1)} all-gather(bf16[1,320,160]{1,2,0:T(8,128)(2,1)S(1)} %bitcast.85), channel_id=1, replica_groups=mesh['dp'=8,'mp'=4] {'mp'}, dimensions={0}, use_global_device_ids=true | all-gather | bytes 512000 | tf_op jit(solution)/shard_map/all_gather | solution.py:273
  60.2 15.7 %all-gather.3 = bf16[4,320,160]{1,2,0:T(8,128)(2,1)S(1)} all-gather(bf16[1,320,160]{1,2,0:T(8,128)(2,1)S(1)} %bitcast.86), channel_id=1, replica_groups=mesh['dp'=8,'mp'=4] {'mp'}, dimensions={0}, use_global_device_ids=true | all-gather | bytes 512000 | tf_op jit(solution)/shard_map/all_gather | solution.py:273
  77.4 16.0 %all-gather.4 = bf16[4,320,160]{1,2,0:T(8,128)(2,1)S(1)} all-gather(bf16[1,320,160]{1,2,0:T(8,128)(2,1)S(1)} %bitcast.87), channel_id=1, replica_groups=mesh['dp'=8,'mp'=4] {'mp'}, dimensions={0}, use_global_device_ids=true | all-gather | bytes 512000 | tf_op jit(solution)/shard_map/all_gather | solution.py:273
  95.7 4.3 collective-permute-start
  100.0 32.0 %all-gather.5 = bf16[4,320,160]{1,2,0:T(8,128)(2,1)S(1)} all-gather(bf16[1,320,160]{1,2,0:T(8,128)(2,1)S(1)} %bitcast.88), channel_id=1, replica_groups=mesh['dp'=8,'mp'=4] {'mp'}, dimensions={0}, use_global_device_ids=true | all-gather | bytes 512000 | tf_op jit(solution)/shard_map/all_gather | solution.py:273
  133.5 4.3 collective-permute-start.1
  140.1 19.0 %all-reduce.1 = f32[1280]{0:T(1024)S(1)} all-reduce(f32[1280]{0:T(1024)S(1)} %dynamic-update-slice), channel_id=1, replica_groups=mesh['dp'=8,'mp'=4] {'mp'}, use_global_device_ids=true, to_apply=%add.1 | all-reduce | flops 1280 | bytes 10240
  159.3 5.9 multiply_convert_fusion.2
  165.2 10.4 %convolution_convert_fusion.6.v_ref = bf16[1536,1280]{1,0:T(8,128)(2,1)} fusion(bf16[1280,1280]{1,0:T(8,128)(2,1)} %all-gather.17.cloned.1.call-done, bf16[512,1280]{1,0:T(8,128)(2,1)S(1)} %copy-done.14, bf16[512,1280]{1,0:T(8,128)(2,1)} %collective-permute-done, bf16[512,1280]{1,0:T(8,128)(2,1)} %collective-permute-done.1), kind=kOutput, calls=%fused_computation.6 | convolution fusion | flops 5046927360 | bytes 11141120 | tf_op jit(solution)/shard_map/dot_general | solution.py:325
  175.6 9.9 %convolution_convert_fusion.7.k_ref = bf16[1536,1280]{1,0:T(8,128)(2,1)} fusion(bf16[1280,1280]{1,0:T(8,128)(2,1)} %all-gather.15.cloned.1.call-done, bf16[512,1280]{1,0:T(8,128)(2,1)S(1)} %copy-done.14, bf16[512,1280]{1,0:T(8,128)(2,1)} %collective-permute-done, bf16[512,1280]{1,0:T(8,128)(2,1)} %collective-permute-done.1), kind=kOutput, calls=%fused_computation.7 | convolution fusion | flops 5046927360 | bytes 11141120 | tf_op jit(solution)/shard_map/dot_general | solution.py:324
  185.5 39.5 %attend_forward.1 = (bf16[512,1280]{1,0:T(8,128)(2,1)S(1)}, f32[16,512]{1,0:T(8,128)S(1)}) custom-call(s32[2]{0:T(128)S(1)} %and_select_fusion.low_ref, bf16[512,1280]{1,0:T(8,128)(2,1)S(1)} %get-tuple-element.37.q_ref, bf16[1536,1280]{1,0:T(8,128)(2,1)} %convolution_convert_fusion.7.k_ref, bf16[1536,1280]{1,0:T(8,128)(2,1)} %convolution_convert_fusion.6.v_ref, ...), custom_call_target="tpu_custom_call" | custom-call | flops 4026531840 | bytes 10485760 | tf_op jit(solution)/shard_map/attend_forward/pallas_call | solution.py:200
  225.6 5.8 multiply_reduce_fusion.2
  231.4 6.3 convolution_add_fusion.5
  237.7 5.2 convert_reduce_fusion.1
  243.9 3.7 convolution_convert_fusion.1
  247.7 5.5 convolution_convert_fusion
  253.3 5.4 multiply_reduce_fusion
  261.0 3.6 convolution_convert_fusion.2
  265.2 4.6 convolution_convert_fusion.8.g_ref
  269.8 2.1 fusion.17.delta_ref
  271.9 52.7 %attend_backward.1 = (bf16[512,1280]{1,0:T(8,128)(2,1)}, bf16[1536,1280]{1,0:T(8,128)(2,1)}, bf16[1536,1280]{1,0:T(8,128)(2,1)}) custom-call(s32[2]{0:T(128)} %copy-done.2, bf16[512,1280]{1,0:T(8,128)(2,1)} %copy-done.3, bf16[1536,1280]{1,0:T(8,128)(2,1)} %convolution_convert_fusion.7.k_ref, bf16[1536,1280]{1,0:T(8,128)(2,1)} %convolution_convert_fusion.6.v_ref, ...), custom_call_target="tpu_custom_call" | custom-call | flops 10066329600 | bytes 15728640 | tf_op jit(solution)/shard_map/attend_backward/pallas_call | solution.py:234
  324.6 9.4 %convolution_convert_fusion.3 = bf16[1280,1280]{1,0:T(8,128)(2,1)} fusion(bf16[1536,1280]{1,0:T(8,128)(2,1)} %get-tuple-element.21, bf16[512,1280]{1,0:T(8,128)(2,1)S(1)} %copy-done.15, bf16[512,1280]{1,0:T(8,128)(2,1)} %collective-permute-done, bf16[512,1280]{1,0:T(8,128)(2,1)} %collective-permute-done.1), kind=kOutput, calls=%fused_computation.3 | convolution fusion | flops 5046599680 | bytes 11141120 | tf_op jit(solution)/shard_map/dot_general | solution.py:23
  334.1 9.6 %convolution_convert_fusion.4 = bf16[1280,1280]{1,0:T(8,128)(2,1)} fusion(bf16[1536,1280]{1,0:T(8,128)(2,1)} %get-tuple-element.20, bf16[512,1280]{1,0:T(8,128)(2,1)S(1)} %copy-done.15, bf16[512,1280]{1,0:T(8,128)(2,1)} %collective-permute-done, bf16[512,1280]{1,0:T(8,128)(2,1)} %collective-permute-done.1), kind=kOutput, calls=%fused_computation.4 | convolution fusion | flops 5046599680 | bytes 11141120 | tf_op jit(solution)/shard_map/dot_general | solution.py:23
  345.0 3.6 convolution_convert_fusion.5
  348.7 4.4 fusion.22
  353.7 2.9 fusion.4
  357.9 4.8 fusion.27
  364.9 4.4 fusion.30
  369.4 3.4 convolution_add_fusion.3
  372.7 4.9 reduce-scatter.35.cloned.1.call-done
  379.8 19.9 %collective-permute-done.2 = bf16[512,1280]{1,0:T(8,128)(2,1)} collective-permute-done((bf16[512,1280]{1,0:T(8,128)(2,1)}, bf16[512,1280]{1,0:T(8,128)(2,1)}, u32[]{:S(2)}, u32[]{:S(2)}) %collective-permute-start.2) | collective-permute-done | bytes 1310752 | tf_op jit(solution)/shard_map/ppermute | solution.py:368
  399.7 6.7 add_convert_fusion
  408.2 19.7 %reduce-scatter.31.cloned.1.call-done = bf16[1280,160]{0,1:T(8,128)(2,1)} async-done(((bf16[1280,1280]{0,1:T(8,128)(2,1)}), bf16[1280,160]{0,1:T(8,128)(2,1)}) %reduce-scatter.31.cloned.1.call-update) | async-done | bytes 409616 | tf_op jit(solution)/shard_map/reduce_scatter | solution.py:279
  430.2 6.9 fusion.2
  437.1 41.0 %reduce-scatter.29.cloned.1.call-done = bf16[160,1280]{1,0:T(8,128)(2,1)} async-done(((bf16[1280,1280]{1,0:T(8,128)(2,1)}), bf16[160,1280]{1,0:T(8,128)(2,1)}) %reduce-scatter.29.cloned.1.call-update) | async-done | bytes 409616 | tf_op jit(solution)/shard_map/reduce_scatter | solution.py:279
  480.5 7.0 fusion.16
  487.5 40.9 %reduce-scatter.27.cloned.1.call-done = bf16[160,1280]{1,0:T(8,128)(2,1)} async-done(((bf16[1280,1280]{1,0:T(8,128)(2,1)}), bf16[160,1280]{1,0:T(8,128)(2,1)}) %reduce-scatter.27.cloned.1.call-update) | async-done | bytes 409616 | tf_op jit(solution)/shard_map/reduce_scatter | solution.py:279
  530.6 39.6 %psum.7 = f32[5200]{0:T(1024)S(1)} all-reduce(f32[5200]{0:T(1024)S(1)} %constant_dynamic-update-slice_fusion), channel_id=1, replica_groups=mesh['dp'=8,'mp'=4] {'dp','mp'}, use_global_device_ids=true, to_apply=%region_21.22 | all-reduce | flops 5200 | bytes 41600 | tf_op jit(solution)/shard_map/psum | solution.py:384
  572.0 6.9 reduce-scatter.25.cloned.1.call-done
  581.0 4.8 fusion.13
  585.8 17.5 %reduce-scatter.45.cloned.1.call-done = bf16[320,160]{1,0:T(8,128)(2,1)} async-done(((bf16[1280,160]{1,0:T(8,128)(2,1)}), bf16[320,160]{1,0:T(8,128)(2,1)}) %reduce-scatter.45.cloned.1.call-update) | async-done | bytes 102416
  605.0 21.5 %reduce-scatter.47.cloned.1.call-done = bf16[320,160]{1,0:T(8,128)(2,1)} async-done(((bf16[1280,160]{1,0:T(8,128)(2,1)}), bf16[320,160]{1,0:T(8,128)(2,1)}) %reduce-scatter.47.cloned.1.call-update) | async-done | bytes 102416
  628.3 21.5 %reduce-scatter.43.cloned.1.call-done = bf16[320,160]{1,0:T(8,128)(2,1)} async-done(((bf16[1280,160]{1,0:T(8,128)(2,1)}), bf16[320,160]{1,0:T(8,128)(2,1)}) %reduce-scatter.43.cloned.1.call-update) | async-done | bytes 102416
  651.5 21.5 %reduce-scatter.41.cloned.1.call-done = bf16[320,160]{1,0:T(8,128)(2,1)} async-done(((bf16[1280,160]{1,0:T(8,128)(2,1)}), bf16[320,160]{1,0:T(8,128)(2,1)}) %reduce-scatter.41.cloned.1.call-update) | async-done | bytes 102416
  674.8 21.5 %reduce-scatter.39.cloned.1.call-done = bf16[320,160]{1,0:T(8,128)(2,1)} async-done(((bf16[1280,160]{1,0:T(8,128)(2,1)}), bf16[320,160]{1,0:T(8,128)(2,1)}) %reduce-scatter.39.cloned.1.call-update) | async-done | bytes 102416
  698.0 21.5 %reduce-scatter.37.cloned.1.call-done = bf16[320,160]{1,0:T(8,128)(2,1)} async-done(((bf16[1280,160]{1,0:T(8,128)(2,1)}), bf16[320,160]{1,0:T(8,128)(2,1)}) %reduce-scatter.37.cloned.1.call-update) | async-done | bytes 102416
  (184 shorter events, 46.7 us)
Async XLA Ops:
  7.2 18.7 %copy-start.19 = (bf16[160,320]{1,0:T(8,128)(2,1)S(1)}, bf16[160,320]{1,0:T(8,128)(2,1)}, u32[]{:S(2)}) copy-start(bf16[160,320]{1,0:T(8,128)(2,1)} %param.18) | copy-start | bytes 307204
  7.2 152.1 %all-gather.13.cloned.1.call-start = ((), (), s32[]{:S(2)}) async-start(), calls=%async_computation.12 | async-start | bytes 3686400 | tf_op jit(solution)/shard_map/all_gather | solution.py:274
  24.4 18.8 %copy-start.20 = (bf16[160,320]{1,0:T(8,128)(2,1)S(1)}, bf16[160,320]{1,0:T(8,128)(2,1)}, u32[]{:S(2)}) copy-start(bf16[160,320]{1,0:T(8,128)(2,1)} %param.17) | copy-start | bytes 307204
  25.9 139.3 %all-gather.17.cloned.1.call-start = ((), (), s32[]{:S(2)}) async-start(), calls=%async_computation.14 | async-start | bytes 3686400 | tf_op jit(solution)/shard_map/all_gather | solution.py:274
  41.8 18.4 %copy-start.21 = (bf16[320,160]{0,1:T(8,128)(2,1)S(1)}, bf16[320,160]{0,1:T(8,128)(2,1)}, u32[]{:S(2)}) copy-start(bf16[320,160]{0,1:T(8,128)(2,1)} %param.19) | copy-start | bytes 307204
  43.2 132.3 %all-gather.15.cloned.1.call-start = ((), (), s32[]{:S(2)}) async-start(), calls=%async_computation.13 | async-start | bytes 3686400 | tf_op jit(solution)/shard_map/all_gather | solution.py:274
  58.7 18.7 %copy-start.22 = (bf16[160,320]{1,0:T(8,128)(2,1)S(1)}, bf16[160,320]{1,0:T(8,128)(2,1)}, u32[]{:S(2)}) copy-start(bf16[160,320]{1,0:T(8,128)(2,1)} %param.20) | copy-start | bytes 307204
  60.1 165.5 %all-gather.19.cloned.1.call-start = ((), (), s32[]{:S(2)}) async-start(), calls=%async_computation.15 | async-start | bytes 3686400 | tf_op jit(solution)/shard_map/all_gather | solution.py:274
  75.9 19.0 %copy-start.5 = (bf16[512,1280]{1,0:T(8,128)(2,1)S(1)}, bf16[512,1280]{1,0:T(8,128)(2,1)}, u32[]{:S(2)}) copy-start(bf16[512,1280]{1,0:T(8,128)(2,1)} %param.14) | copy-start | bytes 3932164
  76.2 19.1 %copy-start.25 = (f32[1280]{0:T(1024)S(1)}, f32[1280]{0:T(1024)}, u32[]{:S(2)}) copy-start(f32[1280]{0:T(1024)} %param.24) | copy-start | bytes 15364
  77.3 154.1 %all-gather.21.cloned.1.call-start = ((), (), s32[]{:S(2)}) async-start(), calls=%async_computation.16 | async-start | bytes 3686400 | tf_op jit(solution)/shard_map/all_gather | solution.py:274
  93.7 6.3 copy-start.23
  94.9 142.8 %all-gather.23.cloned.1.call-start = ((), (), s32[]{:S(2)}) async-start(), calls=%async_computation.17 | async-start | bytes 3686400 | tf_op jit(solution)/shard_map/all_gather | solution.py:274
  95.3 42.5 %copy-start.24 = (s32[1,2048]{1,0:T(1,128)S(1)}, s32[1,2048]{1,0:T(1,128)}, u32[]{:S(2)}) copy-start(s32[1,2048]{1,0:T(1,128)} %param.15) | copy-start | bytes 24580
  95.3 42.7 %copy-start.32 = (f32[80]{0:T(128)S(1)}, f32[80]{0:T(128)}, u32[]{:S(2)}) copy-start(f32[80]{0:T(128)} %param.26) | copy-start | bytes 964
  95.3 43.1 %copy-start.33 = (u32[32]{0:T(128)S(1)}, u32[32]{0:T(128)}, u32[]{:S(2)}) copy-start(u32[32]{0:T(128)} %constant.63) | copy-start | bytes 388
  95.3 44.5 %copy-start.27 = (f32[320]{0:T(512)S(1)}, f32[320]{0:T(512)}, u32[]{:S(2)}) copy-start(f32[320]{0:T(512)} %param.21) | copy-start | bytes 3844
  95.7 42.1 %copy-start.13 = (bf16[512,1280]{1,0:T(8,128)(2,1)}, bf16[512,1280]{1,0:T(8,128)(2,1)S(1)}, u32[]{:S(2)}) copy-start(bf16[512,1280]{1,0:T(8,128)(2,1)S(1)} %fusion.10) | copy-start | bytes 3932164
  95.7 37.7 %collective-permute-start = (bf16[512,1280]{1,0:T(8,128)(2,1)S(1)}, bf16[512,1280]{1,0:T(8,128)(2,1)}, u32[]{:S(2)}, u32[]{:S(2)}) collective-permute-start(bf16[512,1280]{1,0:T(8,128)(2,1)S(1)} %fusion.10), channel_id=1, source_target_pairs={{0,1},{1,2},{2,3},{4,5},{5,6},{6,7},{8,9},{9,10},{10,11},{12,13},{... | collective-permute-start | bytes 3932168 | tf_op jit(solution)/shard_map/ppermute | solution.py:309
  133.4 229.3 %reduce-scatter.33.cloned.1.call-start = ((), (), s32[]{:S(2)}) async-start(), calls=%async_computation.22 | async-start | bytes 3686400 | tf_op jit(solution)/shard_map/reduce_scatter | solution.py:279
  133.5 31.7 %collective-permute-start.1 = (bf16[512,1280]{1,0:T(8,128)(2,1)}, bf16[512,1280]{1,0:T(8,128)(2,1)}, u32[]{:S(2)}, u32[]{:S(2)}) collective-permute-start(bf16[512,1280]{1,0:T(8,128)(2,1)} %collective-permute-done), channel_id=1, source_target_pairs={{0,1},{1,2},{2,3},{4,5},{5,6},{6,7},{8,9},{9,10},{10,11},{12,13},{... | collective-permute-start | bytes 3932168 | tf_op jit(solution)/shard_map/ppermute | solution.py:309
  137.8 47.6 %copy-start.1 = (s32[512]{0:T(512)}, s32[512]{0:T(512)S(1)}, u32[]{:S(2)}) copy-start(s32[512]{0:T(512)S(1)} %pad_dynamic-slice_fusion) | copy-start | bytes 6148
  138.4 47.0 %copy-start = (s32[1536,1]{1,0:T(8,128)}, s32[1536,1]{1,0:T(8,128)S(1)}, u32[]{:S(2)}) copy-start(s32[1536,1]{1,0:T(8,128)S(1)} %broadcast_in_dim.6.seg_key) | copy-start | bytes 18436
  159.2 26.2 %copy-start.2 = (s32[2]{0:T(128)}, s32[2]{0:T(128)S(1)}, u32[]{:S(2)}) copy-start(s32[2]{0:T(128)S(1)} %and_select_fusion.low_ref) | copy-start | bytes 28
  159.2 6.0 copy-start.14
  165.2 20.3 %copy-start.3 = (bf16[512,1280]{1,0:T(8,128)(2,1)}, bf16[512,1280]{1,0:T(8,128)(2,1)S(1)}, u32[]{:S(2)}) copy-start(bf16[512,1280]{1,0:T(8,128)(2,1)S(1)} %get-tuple-element.37.q_ref) | copy-start | bytes 3932164
  225.6 5.8 copy-start.26
  231.4 6.3 copy-start.11
  237.7 6.2 copy-start.8
  247.7 130.0 %reduce-scatter.35.cloned.1.call-start = ((), (), s32[]{:S(2)}) async-start(), calls=%async_computation.23 | async-start | bytes 3686400 | tf_op jit(solution)/shard_map/reduce_scatter | solution.py:279
  253.2 174.8 %reduce-scatter.31.cloned.1.call-start = ((), (), s32[]{:S(2)}) async-start(), calls=%async_computation.21 | async-start | bytes 3686400 | tf_op jit(solution)/shard_map/reduce_scatter | solution.py:279
  264.7 213.4 %reduce-scatter.29.cloned.1.call-start = ((), (), s32[]{:S(2)}) async-start(), calls=%async_computation.20 | async-start | bytes 3686400 | tf_op jit(solution)/shard_map/reduce_scatter | solution.py:279
  271.9 52.7 %copy-start.15 = (bf16[512,1280]{1,0:T(8,128)(2,1)S(1)}, bf16[512,1280]{1,0:T(8,128)(2,1)}, u32[]{:S(2)}) copy-start(bf16[512,1280]{1,0:T(8,128)(2,1)} %copy-done.13) | copy-start | bytes 3932164
  334.0 194.4 %reduce-scatter.27.cloned.1.call-start = ((), (), s32[]{:S(2)}) async-start(), calls=%async_computation.19 | async-start | bytes 3686400 | tf_op jit(solution)/shard_map/reduce_scatter | solution.py:279
  343.6 235.2 %reduce-scatter.25.cloned.1.call-start = ((), (), s32[]{:S(2)}) async-start(), calls=%async_computation.18 | async-start | bytes 3686400 | tf_op jit(solution)/shard_map/reduce_scatter | solution.py:279
  348.6 254.7 %reduce-scatter.45.cloned.1.call-start = ((), (), s32[]{:S(2)}) async-start(), calls=%async_computation.28 | async-start | bytes 819200
  356.6 43.1 %collective-permute-start.2 = (bf16[512,1280]{1,0:T(8,128)(2,1)}, bf16[512,1280]{1,0:T(8,128)(2,1)}, u32[]{:S(2)}, u32[]{:S(2)}) collective-permute-start(bf16[512,1280]{1,0:T(8,128)(2,1)} %fusion.4), channel_id=1, source_target_pairs={{1,0},{2,1},{3,2},{5,4},{6,5},{7,6},{9,8},{10,9},{11,10},{13,12},{... | collective-permute-start | bytes 3932168 | tf_op jit(solution)/shard_map/ppermute | solution.py:368
  364.8 261.7 %reduce-scatter.47.cloned.1.call-start = ((), (), s32[]{:S(2)}) async-start(), calls=%async_computation.29 | async-start | bytes 819200
  379.8 27.9 %copy-start.10 = (f32[512,1280]{1,0:T(8,128)S(1)}, f32[512,1280]{1,0:T(8,128)}, u32[]{:S(2)}) copy-start(f32[512,1280]{1,0:T(8,128)} %get-tuple-element.38) | copy-start | bytes 7864324
  379.8 270.0 %reduce-scatter.43.cloned.1.call-start = ((), (), s32[]{:S(2)}) async-start(), calls=%async_computation.27 | async-start | bytes 819200
  379.8 27.9 %copy-start.17 = (bf16[512,1280]{1,0:T(8,128)(2,1)S(1)}, bf16[512,1280]{1,0:T(8,128)(2,1)}, u32[]{:S(2)}) copy-start(bf16[512,1280]{1,0:T(8,128)(2,1)} %get-tuple-element.22) | copy-start | bytes 3932164
  406.4 74.1 %collective-permute-start.3 = (bf16[512,1280]{1,0:T(8,128)(2,1)}, bf16[512,1280]{1,0:T(8,128)(2,1)}, u32[]{:S(2)}, u32[]{:S(2)}) collective-permute-start(bf16[512,1280]{1,0:T(8,128)(2,1)} %add_convert_fusion), channel_id=1, source_target_pairs={{1,0},{2,1},{3,2},{5,4},{6,5},{7,6},{9,8},{10,9},{11,10},{13,12},{... | collective-permute-start | bytes 3932168 | tf_op jit(solution)/shard_map/ppermute | solution.py:368
  407.7 22.4 %copy-start.31 = (f32[1280]{0:T(1024)S(1)}, f32[1280]{0:T(1024)}, u32[]{:S(2)}) copy-start(f32[1280]{0:T(1024)} %param.23) | copy-start | bytes 15364
  430.1 50.4 %copy-start.6 = (bf16[512,1280]{1,0:T(8,128)(2,1)S(1)}, bf16[512,1280]{1,0:T(8,128)(2,1)}, u32[]{:S(2)}) copy-start(bf16[512,1280]{1,0:T(8,128)(2,1)} %param.14) | copy-start | bytes 3932164
  430.1 50.4 %copy-start.18 = (bf16[512,1280]{1,0:T(8,128)(2,1)S(1)}, bf16[512,1280]{1,0:T(8,128)(2,1)}, u32[]{:S(2)}) copy-start(bf16[512,1280]{1,0:T(8,128)(2,1)} %get-tuple-element.22) | copy-start | bytes 3932164
  430.1 242.9 %reduce-scatter.41.cloned.1.call-start = ((), (), s32[]{:S(2)}) async-start(), calls=%async_computation.26 | async-start | bytes 819200
  480.2 216.0 %reduce-scatter.39.cloned.1.call-start = ((), (), s32[]{:S(2)}) async-start(), calls=%async_computation.25 | async-start | bytes 819200
  530.5 188.9 %reduce-scatter.37.cloned.1.call-start = ((), (), s32[]{:S(2)}) async-start(), calls=%async_computation.24 | async-start | bytes 819200
  (11 other events, 34.6 us)
Sparse Core Ops, SparseCore 0:
  26.0 34.6 all-gather.12
  62.5 32.8 all-gather.16
  97.3 32.8 all-gather.14
  132.0 32.8 all-gather.18
  166.6 32.8 all-gather.20
  201.3 33.1 all-gather.22
  247.8 79.4 reduce-scatter.32
  330.7 46.8 reduce-scatter.34
  381.1 46.8 reduce-scatter.30
  431.2 46.8 reduce-scatter.28
  481.6 46.8 reduce-scatter.26
  531.7 47.0 reduce-scatter.24
  581.1 22.1 reduce-scatter.44
  605.4 21.0 reduce-scatter.46
  628.7 21.0 reduce-scatter.42
  651.9 21.0 reduce-scatter.40
  675.1 21.0 reduce-scatter.38
  698.4 21.0 reduce-scatter.36

commit v2 on v1

v2 whole, which is shorter than its diff:
```python
import functools
import math

import jax
import jax.numpy as jnp
from jax import lax
from jax.experimental import pallas as pl
from jax.experimental.pallas import tpu as pltpu
from jax.sharding import PartitionSpec as P

HD = 80
LANES = 128
EPSILON = 1e-06
LOG2E = 1.442695
DOC_MAX = 1024
FAR = -1e30
F32 = jnp.float32
BF16 = jnp.bfloat16


def dot(a, b, ca, cb):
    return lax.dot_general(a, b, (((ca,), (cb,)), ((), ())), preferred_element_type=F32)


def row_inverse(values):
    return lax.rsqrt(jnp.mean(values * values, axis=1, keepdims=True) + EPSILON)


def spans(rows, width, block):
    own = width - rows
    out=[]
    for qb in range(rows//block):
        hi = own + (qb+1)*block
        lo = max(0, (own + qb*block - (DOC_MAX-1))//block*block)
        out.append((lo,hi))
    return out

def head_lanes(h, features):
    first = h*HD
    off = jnp.minimum(lax.div(first, LANES)*LANES, features-2*LANES)
    off = pl.multiple_of(off, LANES)
    lane = lax.broadcasted_iota(jnp.int32,(1,2*LANES),1) + (off-first)
    return pl.ds(off, 2*LANES), (lane>=0)&(lane<HD)

def fill_bias(seg_query, seg_key, bias, block, own):
    rows = seg_query.shape[1]; width=seg_key.shape[0]
    for kb in range(width//block):
        for qb in range(rows//block):
            row = seg_query[:, qb*block:(qb+1)*block]
            col = seg_key[kb*block:(kb+1)*block,:]
            ahead = (lax.broadcasted_iota(jnp.int32,(block,block),0)+(kb*block)) <= (lax.broadcasted_iota(jnp.int32,(block,block),1)+(own+qb*block))
            bias[kb*block:(kb+1)*block, qb*block:(qb+1)*block] = jnp.where((col==row)&ahead, 0.0, FAR)

def transpose_out(src, dst):
    for i in range(src.shape[0]//LANES):
        at = slice(i*LANES,(i+1)*LANES)
        dst[:, at] = src[at,:].T.astype(dst.dtype)

def forward_kernel(block, q_ref, k_ref, vt_ref, seg_query, seg_key, o_ref, lse_ref, ot, bias, scores, tops):
    rows, features = q_ref.shape; width=k_ref.shape[0]; own=width-rows
    fill_bias(seg_query, seg_key, bias, block, own)
    sp = spans(rows,width,block)
    heads = features//HD
    tiles=[]
    for kb in range(width//block):
        qs=[i for i,(lo,hi) in enumerate(sp) if lo<=kb*block<hi]
        if qs: tiles.append((kb,qs))
    def score(h, slot):
        lanes, mine = head_lanes(h, features)
        query = jnp.where(mine, q_ref[:, lanes], jnp.zeros((), BF16))
        top=[jnp.full((8,block),FAR,F32) for _ in sp]
        for kb,qs in tiles:
            qa, qz = qs[0]*block, (qs[-1]+1)*block
            at = slice(kb*block,(kb+1)*block)
            s = dot(k_ref[at,lanes], query[qa:qz],1,1) + bias[at,qa:qz]
            scores[slot, at, qa:qz] = s
            for i in qs:
                top[i] = jnp.maximum(top[i], jnp.max(s[:, i*block-qa:(i+1)*block-qa].reshape(block//8,8,block),axis=0))
        for i in range(len(sp)):
            tops[slot, :, i*block:(i+1)*block] = jnp.max(top[i],axis=0,keepdims=True)
    def head(h, carry):
        slot = lax.rem(h,2)
        score(h, slot)
        feats = pl.ds(pl.multiple_of(h*HD,16), HD)
        top = tops[slot]
        acc=[jnp.zeros((HD,block),F32) for _ in sp]; total=[jnp.zeros((8,block),F32) for _ in sp]
        for kb,qs in tiles:
            qa, qz = qs[0]*block, (qs[-1]+1)*block
            at = slice(kb*block,(kb+1)*block)
            p = jnp.exp(scores[slot, at, qa:qz] - top[:,qa:qz])
            part = dot(vt_ref[feats,at], p.astype(BF16), 1, 0)
            for i in qs:
                cut = slice(i*block-qa,(i+1)*block-qa)
                total[i] = total[i] + jnp.sum(p[:,cut].reshape(block//8,8,block),axis=0)
                acc[i] = acc[i] + part[:,cut]
        for i in range(len(sp)):
            at = slice(i*block,(i+1)*block)
            one = jnp.sum(total[i],axis=0,keepdims=True)
            ot[feats, at] = acc[i] / one
            lse_ref[pl.ds(h,1), at] = top[:,at] + jnp.log(one)
        return carry
    lax.fori_loop(0, heads, head, 0)
    transpose_out(ot, o_ref)

def attend_forward(q,k,vt,seg_q,seg_k,block):
    rows,features=q.shape; width=k.shape[0]
    return pl.pallas_call(functools.partial(forward_kernel, block),
        out_shape=[jax.ShapeDtypeStruct((rows,features),BF16), jax.ShapeDtypeStruct((features//HD,rows),F32)],
        scratch_shapes=[pltpu.VMEM((features,rows),F32), pltpu.VMEM((width,rows),F32), pltpu.VMEM((2,width,rows),F32), pltpu.VMEM((2,1,rows),F32)],
        compiler_params=pltpu.CompilerParams(vmem_limit_bytes=56<<20), name="attend_forward")(q,k,vt,seg_q,seg_k)

def backward_kernel(block, q_ref,k_ref,kt_ref,v_ref,g_ref,lse_ref,delta_ref,seg_query,seg_key,dq_ref,dk_ref,dv_ref,dqt,bias):
    rows, features = q_ref.shape; width=k_ref.shape[0]; own=width-rows
    fill_bias(seg_query, seg_key, bias, block, own)
    dk_ref[...] = jnp.zeros_like(dk_ref); dv_ref[...] = jnp.zeros_like(dv_ref)
    sp = spans(rows,width,block)
    def head(h, carry):
        lanes, mine = head_lanes(h, features)
        feats = pl.ds(pl.multiple_of(h*HD,16), HD)
        zero = jnp.zeros((), BF16)
        query = jnp.where(mine, q_ref[:, lanes], zero)
        grad = jnp.where(mine, g_ref[:, lanes], zero)
        lse = lse_ref[pl.ds(h,1),:]; delta=delta_ref[pl.ds(h,1),:]
        acc = [jnp.zeros((HD,block),F32) for _ in sp]
        for kb in range(width//block):
            qs=[i for i,(lo,hi) in enumerate(sp) if lo<=kb*block<hi]
            if not qs: continue
            qa, qz = qs[0]*block, (qs[-1]+1)*block
            at = slice(kb*block,(kb+1)*block)
            s = dot(k_ref[at,lanes], query[qa:qz],1,1) + bias[at,qa:qz]
            p = jnp.exp(s - lse[:,qa:qz])
            dp = dot(v_ref[at,lanes], grad[qa:qz],1,1)
            ds = (p*(dp-delta[:,qa:qz])).astype(BF16)
            dv_ref[at,lanes] += dot(p.astype(BF16), grad[qa:qz],1,0).astype(BF16)
            dk_ref[at,lanes] += dot(ds, query[qa:qz],1,0).astype(BF16)
            part = dot(kt_ref[feats,at], ds, 1, 0)
            for i in qs:
                acc[i] = acc[i] + part[:, i*block-qa:(i+1)*block-qa]
        for i in range(len(sp)):
            dqt[feats, i*block:(i+1)*block] = acc[i]
        return carry
    lax.fori_loop(0, features//HD, head, 0)
    transpose_out(dqt, dq_ref)

def attend_backward(q,k,kt,v,g,lse,delta,seg_q,seg_k,block):
    rows,features=q.shape; width=k.shape[0]
    return pl.pallas_call(functools.partial(backward_kernel, block),
        out_shape=[jax.ShapeDtypeStruct((rows,features),BF16), jax.ShapeDtypeStruct((width,features),BF16), jax.ShapeDtypeStruct((width,features),BF16)],
        scratch_shapes=[pltpu.VMEM((features,rows),F32), pltpu.VMEM((width,rows),F32)],
        compiler_params=pltpu.CompilerParams(vmem_limit_bytes=60<<20), name="attend_backward")(q,k,kt,v,g,lse,delta,seg_q,seg_k)

def gather_weight(block, row_axis, col_axis):
    wide = lax.all_gather(block, "mp", axis=1 if col_axis == "mp" else 0, tiled=True)
    return lax.all_gather(wide, "dp", axis=1 if col_axis == "dp" else 0, tiled=True)


def scatter_grad(grad, row_axis, col_axis):
    low = grad.astype(BF16)
    mine = lax.psum_scatter(low, "dp", scatter_dimension=1 if col_axis == "dp" else 0, tiled=True)
    mine = lax.psum_scatter(mine, "mp", scatter_dimension=1 if col_axis == "mp" else 0, tiled=True)
    return mine.astype(F32)


def body(
    tokens, segments, w_query, w_key, w_value, w_output, w_up, b_up, w_down, b_down,
    gain_attn, gain_mlp, query_scale, cotangent,
):
    stages = lax.axis_size("mp")
    z = lax.axis_index("mp")
    seg = segments[0]
    rows, features = tokens.shape
    back = min(stages - 1, -(-(DOC_MAX - 1) // rows))
    own = back * rows
    block = min(256, rows)
    up = [(i, i + 1) for i in range(stages - 1)]
    down = [(i + 1, i) for i in range(stages - 1)]

    wq, wk, wv, wu = (
        gather_weight(w, "dp", "mp") for w in (w_query, w_key, w_value, w_up)
    )
    wo, wd = (gather_weight(w, "mp", "dp") for w in (w_output, w_down))
    b_full = lax.all_gather(b_up, "mp", axis=0, tiled=True)

    inputs = tokens.astype(F32)
    inv_first = row_inverse(inputs)
    normed = (inputs * inv_first * gain_attn).astype(BF16)
    window = [normed]
    for _ in range(back):
        window.append(lax.ppermute(window[-1], "mp", up))
    first = jnp.concatenate(window[::-1], axis=0)

    seg_wide = jnp.concatenate([jnp.full((own,), -1, jnp.int32), seg])
    seg_window = lax.dynamic_slice_in_dim(seg_wide, z * rows, own + rows, 0)
    seg_query = seg_window[own:]
    seg_query, seg_key = seg_query[None, :], seg_window[:, None]

    heads = features // HD
    factor = jax.nn.softplus(query_scale) * (LOG2E / math.sqrt(HD))
    factor_cols = jnp.tile(factor, heads)
    query_raw = jnp.dot(normed, wq, preferred_element_type=F32)
    scaled = (query_raw * factor_cols).astype(BF16)
    keys = jnp.dot(first, wk, preferred_element_type=F32).astype(BF16)
    values = jnp.dot(first, wv, preferred_element_type=F32).astype(BF16)
    mixed, lse = attend_forward(scaled, keys, values.T, seg_query, seg_key, block)

    hidden = inputs + jnp.dot(mixed, wo, preferred_element_type=F32)
    inv_second = row_inverse(hidden)
    second = (hidden * inv_second * gain_mlp).astype(BF16)
    preact = jnp.dot(second, wu, preferred_element_type=F32) + b_full
    active = jax.nn.silu(preact).astype(BF16)
    layer_out = (hidden + jnp.dot(active, wd, preferred_element_type=F32) + b_down).astype(BF16)

    upstream = cotangent.astype(F32)
    sigma = jax.nn.sigmoid(preact)
    d_active = dot(cotangent, wd, 1, 1)
    d_preact = (d_active * sigma * (1.0 + preact * (1.0 - sigma))).astype(BF16)
    d_second = dot(d_preact, wu, 1, 1)
    weighted = d_second * gain_mlp
    dots = jnp.sum(weighted * hidden, axis=1, keepdims=True)
    cube = inv_second * inv_second * inv_second
    d_hidden = upstream + inv_second * weighted - hidden * cube / features * dots
    d_attn = d_hidden.astype(BF16)
    d_mixed = dot(d_attn, wo, 1, 1).astype(BF16)

    owner = (jnp.arange(features)[None, :] // HD == jnp.arange(heads)[:, None]).astype(F32)
    delta = lax.dot_general(
        owner, d_mixed.astype(F32) * mixed.astype(F32), (((1,), (1,)), ((), ())),
        precision=lax.Precision.HIGHEST, preferred_element_type=F32,
    )
    d_scaled, d_keys, d_values = attend_backward(
        scaled, keys, keys.T, values, d_mixed, lse, delta, seg_query, seg_key, block
    )
    d_scaled_wide = d_scaled.astype(F32)
    d_query = (d_scaled_wide * factor_cols).astype(BF16)
    scale_part = jnp.sum(jnp.sum(d_scaled_wide * query_raw, axis=0).reshape(heads, HD), axis=0)

    part = None
    for c in range(back + 1):
        at = slice(c * rows, (c + 1) * rows)
        term = dot(d_keys[at], wk, 1, 1) + dot(d_values[at], wv, 1, 1)
        if c == back:
            term = term + dot(d_query, wq, 1, 1)
        if part is not None:
            term = term + part
        if c < back:
            part = lax.ppermute(term.astype(BF16), "mp", down).astype(F32)
    d_first = term

    weighted_first = d_first * gain_attn
    cube_first = inv_first * inv_first * inv_first
    first_dots = jnp.sum(weighted_first * inputs, axis=1, keepdims=True)
    tokens_grad = (
        d_hidden + inv_first * weighted_first - inputs * cube_first / features * first_dots
    ).astype(BF16)

    grad_gain_attn = jnp.sum(d_first * inputs * inv_first, axis=0)
    grad_gain_mlp = jnp.sum(d_second * hidden * inv_second, axis=0)
    grad_b_up = jnp.sum(d_preact.astype(F32), axis=0)
    sums = jnp.concatenate(
        [grad_gain_mlp, jnp.sum(upstream, axis=0), grad_b_up, grad_gain_attn, scale_part]
    )
    sums = lax.psum(sums, ("dp", "mp"))
    sum_gain_mlp, sum_b_down, sum_b_up, sum_gain_attn, scale_total = jnp.split(
        sums, [features, 2 * features, 3 * features, 4 * features]
    )
    mine = b_up.shape[0]
    sum_b_up = lax.dynamic_slice_in_dim(sum_b_up, z * mine, mine, 0)
    grad_query_scale = scale_total * (LOG2E / math.sqrt(HD)) * jax.nn.sigmoid(query_scale)

    grads = (
        scatter_grad(dot(normed, d_query, 0, 0), "dp", "mp"),
        scatter_grad(dot(first, d_keys, 0, 0), "dp", "mp"),
        scatter_grad(dot(first, d_values, 0, 0), "dp", "mp"),
        scatter_grad(dot(mixed, d_attn, 0, 0), "mp", "dp"),
        scatter_grad(dot(second, d_preact, 0, 0), "dp", "mp"),
        scatter_grad(dot(active, cotangent, 0, 0), "mp", "dp"),
    )
    return (
        layer_out, tokens_grad, grads[0], grads[1], grads[2], grads[3], grads[4], sum_b_up,
        grads[5], sum_b_down, sum_gain_attn, sum_gain_mlp, grad_query_scale,
    )


def solution(mesh):
    tokens, rows_dp, rows_mp = P(("dp", "mp"), None), P("dp", "mp"), P("mp", "dp")
    return jax.shard_map(
        body,
        mesh=mesh,
        in_specs=(
            tokens, P("dp", None), rows_dp, rows_dp, rows_dp, rows_mp, rows_dp, P("mp"), rows_mp,
            P(), P(), P(), P(), tokens,
        ),
        out_specs=(
            tokens, tokens, rows_dp, rows_dp, rows_dp, rows_mp, rows_dp, P("mp"), rows_mp,
            P(), P(), P(), P(),
        ),
        check_vma=False,
    )
```

time: 734 us -> 702 us (0.956)
  waiting for transfers between devices: 259 us -> 233 us
  Pallas kernels: 92.2 us -> 70.1 us
  local copies, waits for them, and re-layouts: 35.3 us -> 47.6 us
    pallas_call x2, Pallas kernels: 92.2 us -> 70.1 us  [the longest x1 45.1 us: attend_backward(): pl.pallas_call(functools.partial(backward_kernel, block), out_shape=[jax....]
    reduce_scatter x6, waiting for transfers between devices: 114 us -> 93.9 us  [scatter_grad(): lax.psum_scatter(low, 'dp', scatter_dimension=1 if col_axis == 'dp' else...]
    convert_element_type x0 -> x2, local copies, waits for them, and re-layouts: none -> 12.7 us  [the longest x1 6.42 us: body(): keys = jnp.dot(first, wk, preferred_element_type=F32).astype(BF16)]
    unnamed x99 -> x85, local copies, waits for them, and re-layouts: 31.8 us -> 30 us
  transfers between devices with their start and end apart: 22 -> 22, of which waited for: 12 -> 11; matrix products, arithmetic and copies ran while one was open for 22% -> 25% of each run, Pallas kernels for 13% -> 10%
where the time goes in v2:
time: 702 us; the launch traced here: 693 us
  waiting for transfers between devices  233 us (33%)
  blocking collectives  169 us (24%)
  matrix products  133 us (19%)
  Pallas kernels  70.1 us (10%)
  local copies, waits for them, and re-layouts  47.6 us (7%)
  between operations  16 us (2%)
  starting transfers between devices  12.7 us (2%)
  other arithmetic  11.6 us (2%)
    unnamed x24, waiting for transfers between devices  125 us
    all_gather x6, blocking collectives, gather_weight(): lax.all_gather(block, 'mp', axis=1 if col_axis == 'mp' else 0, tiled=True)  112 us
    reduce_scatter x6, waiting for transfers between devices, scatter_grad(): lax.psum_scatter(low, 'dp', scatter_dimension=1 if col_axis == 'dp' else...  93.9 us
    dot_general x16, matrix products, dot(): lax.dot_general(a, b, (((ca,), (cb,)), ((), ())), preferred_element_type=...  85.9 us
    pallas_call x1, Pallas kernels, attend_backward(): pl.pallas_call(functools.partial(backward_kernel, block), out_shape=[jax....  45.1 us
    psum x1, blocking collectives, body(): sums = lax.psum(sums, ('dp', 'mp'))  39.6 us
    unnamed x85, local copies, waits for them, and re-layouts  30 us
    pallas_call x1, Pallas kernels, attend_forward(): pl.pallas_call(functools.partial(forward_kernel, block), out_shape=[jax.S...  25 us
  transfers between devices with their start and end apart: 22, of which 11 were waited for; matrix products, arithmetic and copies ran while one was open for 25% of the time, Pallas kernels for 10%

profile of v2, /device:TPU:0, one launch (start us, length us, event | category | flops | bytes accessed | tf_op | source)
XLA Modules:
  0.0 693.0 jit_solution(16631141287421135280)
XLA Ops:
  7.2 17.2 %all-gather.1 = bf16[4,320,160]{1,2,0:T(8,128)(2,1)S(1)} all-gather(bf16[1,320,160]{1,2,0:T(8,128)(2,1)} %bitcast.85), channel_id=1, replica_groups=mesh['dp'=8,'mp'=4] {'mp'}, dimensions={0}, use_global_device_ids=true | all-gather | bytes 512000 | tf_op jit(solution)/shard_map/all_gather | solution.py:153
  25.9 15.9 %all-gather.2 = bf16[4,320,160]{1,2,0:T(8,128)(2,1)S(1)} all-gather(bf16[1,320,160]{1,2,0:T(8,128)(2,1)S(1)} %bitcast.86), channel_id=1, replica_groups=mesh['dp'=8,'mp'=4] {'mp'}, dimensions={0}, use_global_device_ids=true | all-gather | bytes 512000 | tf_op jit(solution)/shard_map/all_gather | solution.py:153
  43.3 15.4 %all-gather = bf16[4,320,160]{1,2,0:T(8,128)(2,1)S(1)} all-gather(bf16[1,320,160]{1,2,0:T(8,128)(2,1)S(1)} %bitcast.87), channel_id=1, replica_groups=mesh['dp'=8,'mp'=4] {'mp'}, dimensions={0}, use_global_device_ids=true | all-gather | bytes 512000 | tf_op jit(solution)/shard_map/all_gather | solution.py:153
  60.2 15.7 %all-gather.3 = bf16[4,320,160]{1,2,0:T(8,128)(2,1)S(1)} all-gather(bf16[1,320,160]{1,2,0:T(8,128)(2,1)S(1)} %bitcast.88), channel_id=1, replica_groups=mesh['dp'=8,'mp'=4] {'mp'}, dimensions={0}, use_global_device_ids=true | all-gather | bytes 512000 | tf_op jit(solution)/shard_map/all_gather | solution.py:153
  77.5 15.9 %all-gather.4 = bf16[4,320,160]{1,2,0:T(8,128)(2,1)S(1)} all-gather(bf16[1,320,160]{1,2,0:T(8,128)(2,1)S(1)} %bitcast.89), channel_id=1, replica_groups=mesh['dp'=8,'mp'=4] {'mp'}, dimensions={0}, use_global_device_ids=true | all-gather | bytes 512000 | tf_op jit(solution)/shard_map/all_gather | solution.py:153
  95.6 4.5 collective-permute-start
  100.1 32.0 %all-gather.5 = bf16[4,320,160]{1,2,0:T(8,128)(2,1)S(1)} all-gather(bf16[1,320,160]{1,2,0:T(8,128)(2,1)S(1)} %bitcast.90), channel_id=1, replica_groups=mesh['dp'=8,'mp'=4] {'mp'}, dimensions={0}, use_global_device_ids=true | all-gather | bytes 512000 | tf_op jit(solution)/shard_map/all_gather | solution.py:153
  133.6 4.3 collective-permute-start.1
  140.8 17.8 %all-reduce.1 = f32[1280]{0:T(1024)S(1)} all-reduce(f32[1280]{0:T(1024)S(1)} %dynamic-update-slice), channel_id=1, replica_groups=mesh['dp'=8,'mp'=4] {'mp'}, use_global_device_ids=true, to_apply=%add.1 | all-reduce | flops 1280 | bytes 10240
  159.3 10.0 %convolution_convert_fusion.7 = bf16[1536,1280]{0,1:T(8,128)(2,1)} fusion(bf16[1280,1280]{1,0:T(8,128)(2,1)} %all-gather.15.cloned.1.call-done, bf16[512,1280]{1,0:T(8,128)(2,1)S(1)} %fusion.10, bf16[512,1280]{1,0:T(8,128)(2,1)} %collective-permute-done, bf16[512,1280]{1,0:T(8,128)(2,1)} %collective-permute-done.1), kind=kOutput, calls=%fused_computation.7 | convolution fusion | flops 5046927360 | bytes 11141120 | tf_op jit(solution)/shard_map/dot_general | solution.py:202
  169.3 6.4 copy.59.k_ref
  175.7 9.9 %convolution_convert_fusion.6.v_ref = bf16[1536,1280]{1,0:T(8,128)(2,1)} fusion(bf16[1280,1280]{1,0:T(8,128)(2,1)} %all-gather.17.cloned.1.call-done, bf16[512,1280]{1,0:T(8,128)(2,1)S(1)} %fusion.10, bf16[512,1280]{1,0:T(8,128)(2,1)} %collective-permute-done, bf16[512,1280]{1,0:T(8,128)(2,1)} %collective-permute-done.1), kind=kOutput, calls=%fused_computation.6 | convolution fusion | flops 5046927360 | bytes 11141120 | tf_op jit(solution)/shard_map/dot_general | solution.py:203
  185.6 6.3 copy.60.vt_ref
  191.9 5.8 multiply_convert_fusion.2
  197.7 25.0 %attend_forward.1 = (bf16[512,1280]{1,0:T(8,128)(2,1)}, f32[16,512]{1,0:T(8,128)}) custom-call(bf16[512,1280]{1,0:T(8,128)(2,1)} %get-tuple-element.37.q_ref, bf16[1536,1280]{1,0:T(8,128)(2,1)} %copy.59.k_ref, bf16[1280,1536]{1,0:T(8,128)(2,1)} %copy.60.vt_ref, s32[1,512]{1,0:T(1,128)} %bitcast.93, s32[1536,1]{1,0:T(8,128)} %broadcast_in_dim.6.seg_key), custom_call_target="tpu_custom_call" | custom-call | tf_op jit(solution)/shard_map/attend_forward/pallas_call | solution.py:107
  222.7 5.8 multiply_reduce_fusion.2
  228.5 6.3 convolution_add_fusion.5
  234.8 5.2 convert_reduce_fusion.1
  241.1 3.7 convolution_convert_fusion.1
  244.9 5.4 convolution_convert_fusion
  250.4 5.9 multiply_reduce_fusion
  258.6 3.6 convolution_convert_fusion.2
  262.5 4.7 convolution_convert_fusion.8.g_ref
  269.3 45.1 %attend_backward.1 = (bf16[512,1280]{1,0:T(8,128)(2,1)}, bf16[1536,1280]{1,0:T(8,128)(2,1)}, bf16[1536,1280]{1,0:T(8,128)(2,1)}) custom-call(bf16[512,1280]{1,0:T(8,128)(2,1)} %get-tuple-element.37.q_ref, bf16[1536,1280]{1,0:T(8,128)(2,1)} %copy.59.k_ref, bf16[1280,1536]{1,0:T(8,128)(2,1)} %bitcast.71, bf16[1536,1280]{1,0:T(8,128)(2,1)} %convolution_convert_fusion.6.v_ref, ...), custom_call_target="tpu_custom_call" | custom-call | tf_op jit(solution)/shard_map/attend_backward/pallas_call | solution.py:147
  314.4 9.4 %convolution_convert_fusion.3 = bf16[1280,1280]{1,0:T(8,128)(2,1)} fusion(bf16[1536,1280]{1,0:T(8,128)(2,1)} %get-tuple-element.21, bf16[512,1280]{1,0:T(8,128)(2,1)S(1)} %copy-done.10, bf16[512,1280]{1,0:T(8,128)(2,1)} %collective-permute-done, bf16[512,1280]{1,0:T(8,128)(2,1)} %collective-permute-done.1), kind=kOutput, calls=%fused_computation.3 | convolution fusion | flops 5046599680 | bytes 11141120 | tf_op jit(solution)/shard_map/dot_general | solution.py:22
  323.9 9.4 %convolution_convert_fusion.4 = bf16[1280,1280]{1,0:T(8,128)(2,1)} fusion(bf16[1536,1280]{1,0:T(8,128)(2,1)} %get-tuple-element.20, bf16[512,1280]{1,0:T(8,128)(2,1)S(1)} %copy-done.10, bf16[512,1280]{1,0:T(8,128)(2,1)} %collective-permute-done, bf16[512,1280]{1,0:T(8,128)(2,1)} %collective-permute-done.1), kind=kOutput, calls=%fused_computation.4 | convolution fusion | flops 5046599680 | bytes 11141120 | tf_op jit(solution)/shard_map/dot_general | solution.py:22
  333.5 5.2 convolution_convert_fusion.5
  338.8 4.4 fusion.22
  343.4 3.0 fusion.4
  347.7 4.7 fusion.27
  354.6 4.7 fusion.30
  359.8 3.4 convolution_add_fusion.3
  365.3 14.1 %collective-permute-done.2 = bf16[512,1280]{1,0:T(8,128)(2,1)} collective-permute-done((bf16[512,1280]{1,0:T(8,128)(2,1)}, bf16[512,1280]{1,0:T(8,128)(2,1)}, u32[]{:S(2)}, u32[]{:S(2)}) %collective-permute-start.2) | collective-permute-done | bytes 1310752 | tf_op jit(solution)/shard_map/ppermute | solution.py:246
  379.4 6.5 add_convert_fusion
  387.7 4.8 reduce-scatter.31.cloned.1.call-done
  394.7 6.8 fusion.2
  401.5 41.2 %reduce-scatter.29.cloned.1.call-done = bf16[160,1280]{1,0:T(8,128)(2,1)} async-done(((bf16[1280,1280]{1,0:T(8,128)(2,1)}), bf16[160,1280]{1,0:T(8,128)(2,1)}) %reduce-scatter.29.cloned.1.call-update) | async-done | bytes 409616 | tf_op jit(solution)/shard_map/reduce_scatter | solution.py:159
  445.1 7.0 %fusion.16 = (f32[1280]{0:T(1024)S(1)}, f32[512]{0:T(512)S(1)}, f32[512,1280]{1,0:T(8,128)}) fusion(bf16[512,1280]{1,0:T(8,128)(2,1)S(1)} %copy-done, f32[512]{0:T(512)S(1)} %get-tuple-element.34, bf16[512,1280]{1,0:T(8,128)(2,1)} %collective-permute-done.3, f32[1280]{0:T(1024)S(1)} %copy-done.18, f32[512,1280]{1,0:T(8,128)} %convolution_add_fusion.3, ...), kind=kOutput, calls=%fused_computation.43 | convolution fusion | flops 1686239488 | bytes 12471296 | tf_op jit(solution)/shard_map/dot_general | solution.py:22
  452.1 41.0 %reduce-scatter.27.cloned.1.call-done = bf16[160,1280]{1,0:T(8,128)(2,1)} async-done(((bf16[1280,1280]{1,0:T(8,128)(2,1)}), bf16[160,1280]{1,0:T(8,128)(2,1)}) %reduce-scatter.27.cloned.1.call-update) | async-done | bytes 409616 | tf_op jit(solution)/shard_map/reduce_scatter | solution.py:159
  495.2 39.6 %psum.7 = f32[5200]{0:T(1024)S(1)} all-reduce(f32[5200]{0:T(1024)S(1)} %constant_dynamic-update-slice_fusion), channel_id=1, replica_groups=mesh['dp'=8,'mp'=4] {'dp','mp'}, use_global_device_ids=true, to_apply=%region_20.21 | all-reduce | flops 5200 | bytes 41600 | tf_op jit(solution)/shard_map/psum | solution.py:262
  536.6 6.9 reduce-scatter.25.cloned.1.call-done
  545.6 4.8 fusion.13
  550.4 17.5 %reduce-scatter.45.cloned.1.call-done = bf16[320,160]{1,0:T(8,128)(2,1)} async-done(((bf16[1280,160]{1,0:T(8,128)(2,1)}), bf16[320,160]{1,0:T(8,128)(2,1)}) %reduce-scatter.45.cloned.1.call-update) | async-done | bytes 102416
  569.6 21.5 %reduce-scatter.47.cloned.1.call-done = bf16[320,160]{1,0:T(8,128)(2,1)} async-done(((bf16[1280,160]{1,0:T(8,128)(2,1)}), bf16[320,160]{1,0:T(8,128)(2,1)}) %reduce-scatter.47.cloned.1.call-update) | async-done | bytes 102416
  592.8 21.4 %reduce-scatter.43.cloned.1.call-done = bf16[320,160]{1,0:T(8,128)(2,1)} async-done(((bf16[1280,160]{1,0:T(8,128)(2,1)}), bf16[320,160]{1,0:T(8,128)(2,1)}) %reduce-scatter.43.cloned.1.call-update) | async-done | bytes 102416
  616.1 21.5 %reduce-scatter.41.cloned.1.call-done = bf16[320,160]{1,0:T(8,128)(2,1)} async-done(((bf16[1280,160]{1,0:T(8,128)(2,1)}), bf16[320,160]{1,0:T(8,128)(2,1)}) %reduce-scatter.41.cloned.1.call-update) | async-done | bytes 102416
  639.3 21.4 %reduce-scatter.39.cloned.1.call-done = bf16[320,160]{1,0:T(8,128)(2,1)} async-done(((bf16[1280,160]{1,0:T(8,128)(2,1)}), bf16[320,160]{1,0:T(8,128)(2,1)}) %reduce-scatter.39.cloned.1.call-update) | async-done | bytes 102416
  662.5 21.5 %reduce-scatter.37.cloned.1.call-done = bf16[320,160]{1,0:T(8,128)(2,1)} async-done(((bf16[1280,160]{1,0:T(8,128)(2,1)}), bf16[320,160]{1,0:T(8,128)(2,1)}) %reduce-scatter.37.cloned.1.call-update) | async-done | bytes 102416
  (169 shorter events, 48.0 us)
Async XLA Ops:
  7.2 18.7 %copy-start.12 = (bf16[160,320]{1,0:T(8,128)(2,1)S(1)}, bf16[160,320]{1,0:T(8,128)(2,1)}, u32[]{:S(2)}) copy-start(bf16[160,320]{1,0:T(8,128)(2,1)} %param.18) | copy-start | bytes 307204
  7.2 152.1 %all-gather.15.cloned.1.call-start = ((), (), s32[]{:S(2)}) async-start(), calls=%async_computation.13 | async-start | bytes 3686400 | tf_op jit(solution)/shard_map/all_gather | solution.py:154
  24.4 18.9 %copy-start.13 = (bf16[160,320]{1,0:T(8,128)(2,1)S(1)}, bf16[160,320]{1,0:T(8,128)(2,1)}, u32[]{:S(2)}) copy-start(bf16[160,320]{1,0:T(8,128)(2,1)} %param.16) | copy-start | bytes 307204
  25.9 149.8 %all-gather.17.cloned.1.call-start = ((), (), s32[]{:S(2)}) async-start(), calls=%async_computation.14 | async-start | bytes 3686400 | tf_op jit(solution)/shard_map/all_gather | solution.py:154
  41.8 18.4 %copy-start.14 = (bf16[320,160]{0,1:T(8,128)(2,1)S(1)}, bf16[320,160]{0,1:T(8,128)(2,1)}, u32[]{:S(2)}) copy-start(bf16[320,160]{0,1:T(8,128)(2,1)} %param.19) | copy-start | bytes 307204
  43.2 148.7 %all-gather.13.cloned.1.call-start = ((), (), s32[]{:S(2)}) async-start(), calls=%async_computation.12 | async-start | bytes 3686400 | tf_op jit(solution)/shard_map/all_gather | solution.py:154
  58.7 18.8 %copy-start.15 = (bf16[160,320]{1,0:T(8,128)(2,1)S(1)}, bf16[160,320]{1,0:T(8,128)(2,1)}, u32[]{:S(2)}) copy-start(bf16[160,320]{1,0:T(8,128)(2,1)} %param.20) | copy-start | bytes 307204
  60.1 162.5 %all-gather.19.cloned.1.call-start = ((), (), s32[]{:S(2)}) async-start(), calls=%async_computation.15 | async-start | bytes 3686400 | tf_op jit(solution)/shard_map/all_gather | solution.py:154
  75.9 18.9 %copy-start = (bf16[512,1280]{1,0:T(8,128)(2,1)S(1)}, bf16[512,1280]{1,0:T(8,128)(2,1)}, u32[]{:S(2)}) copy-start(bf16[512,1280]{1,0:T(8,128)(2,1)} %param.14) | copy-start | bytes 3932164
  76.2 19.0 %copy-start.18 = (f32[1280]{0:T(1024)S(1)}, f32[1280]{0:T(1024)}, u32[]{:S(2)}) copy-start(f32[1280]{0:T(1024)} %param.24) | copy-start | bytes 15364
  77.4 151.1 %all-gather.21.cloned.1.call-start = ((), (), s32[]{:S(2)}) async-start(), calls=%async_computation.16 | async-start | bytes 3686400 | tf_op jit(solution)/shard_map/all_gather | solution.py:154
  93.6 6.5 copy-start.16
  94.8 140.0 %all-gather.23.cloned.1.call-start = ((), (), s32[]{:S(2)}) async-start(), calls=%async_computation.17 | async-start | bytes 3686400 | tf_op jit(solution)/shard_map/all_gather | solution.py:154
  95.2 42.7 %copy-start.27 = (f32[80]{0:T(128)S(1)}, f32[80]{0:T(128)}, u32[]{:S(2)}) copy-start(f32[80]{0:T(128)} %param.26) | copy-start | bytes 964
  95.2 42.8 %copy-start.17 = (s32[1,2048]{1,0:T(1,128)S(1)}, s32[1,2048]{1,0:T(1,128)}, u32[]{:S(2)}) copy-start(s32[1,2048]{1,0:T(1,128)} %param.15) | copy-start | bytes 24580
  95.2 44.0 %copy-start.28 = (u32[32]{0:T(128)S(1)}, u32[32]{0:T(128)}, u32[]{:S(2)}) copy-start(u32[32]{0:T(128)} %constant.50) | copy-start | bytes 388
  95.3 45.3 %copy-start.20 = (f32[320]{0:T(512)S(1)}, f32[320]{0:T(512)}, u32[]{:S(2)}) copy-start(f32[320]{0:T(512)} %param.21) | copy-start | bytes 3844
  95.6 96.3 %copy-start.9 = (bf16[512,1280]{1,0:T(8,128)(2,1)}, bf16[512,1280]{1,0:T(8,128)(2,1)S(1)}, u32[]{:S(2)}) copy-start(bf16[512,1280]{1,0:T(8,128)(2,1)S(1)} %fusion.10) | copy-start | bytes 3932164
  95.6 37.9 %collective-permute-start = (bf16[512,1280]{1,0:T(8,128)(2,1)S(1)}, bf16[512,1280]{1,0:T(8,128)(2,1)}, u32[]{:S(2)}, u32[]{:S(2)}) collective-permute-start(bf16[512,1280]{1,0:T(8,128)(2,1)S(1)} %fusion.10), channel_id=1, source_target_pairs={{0,1},{1,2},{2,3},{4,5},{5,6},{6,7},{8,9},{9,10},{10,11},{12,13},{... | collective-permute-start | bytes 3932168 | tf_op jit(solution)/shard_map/ppermute | solution.py:189
  133.5 218.8 %reduce-scatter.33.cloned.1.call-start = ((), (), s32[]{:S(2)}) async-start(), calls=%async_computation.22 | async-start | bytes 3686400 | tf_op jit(solution)/shard_map/reduce_scatter | solution.py:159
  133.6 25.7 %collective-permute-start.1 = (bf16[512,1280]{1,0:T(8,128)(2,1)}, bf16[512,1280]{1,0:T(8,128)(2,1)}, u32[]{:S(2)}, u32[]{:S(2)}) collective-permute-start(bf16[512,1280]{1,0:T(8,128)(2,1)} %collective-permute-done), channel_id=1, source_target_pairs={{0,1},{1,2},{2,3},{4,5},{5,6},{6,7},{8,9},{9,10},{10,11},{12,13},{... | collective-permute-start | bytes 3932168 | tf_op jit(solution)/shard_map/ppermute | solution.py:189
  222.7 5.8 copy-start.19
  228.5 6.3 copy-start.6
  234.8 6.3 copy-start.3
  244.9 118.2 %reduce-scatter.35.cloned.1.call-start = ((), (), s32[]{:S(2)}) async-start(), calls=%async_computation.23 | async-start | bytes 3686400 | tf_op jit(solution)/shard_map/reduce_scatter | solution.py:159
  250.3 142.2 %reduce-scatter.31.cloned.1.call-start = ((), (), s32[]{:S(2)}) async-start(), calls=%async_computation.21 | async-start | bytes 3686400 | tf_op jit(solution)/shard_map/reduce_scatter | solution.py:159
  250.4 5.9 copy-start.4
  262.2 180.5 %reduce-scatter.29.cloned.1.call-start = ((), (), s32[]{:S(2)}) async-start(), calls=%async_computation.20 | async-start | bytes 3686400 | tf_op jit(solution)/shard_map/reduce_scatter | solution.py:159
  262.5 4.7 copy-start.8
  269.3 45.1 %copy-start.10 = (bf16[512,1280]{1,0:T(8,128)(2,1)S(1)}, bf16[512,1280]{1,0:T(8,128)(2,1)}, u32[]{:S(2)}) copy-start(bf16[512,1280]{1,0:T(8,128)(2,1)} %copy-done.9) | copy-start | bytes 3932164
  323.8 169.2 %reduce-scatter.27.cloned.1.call-start = ((), (), s32[]{:S(2)}) async-start(), calls=%async_computation.19 | async-start | bytes 3686400 | tf_op jit(solution)/shard_map/reduce_scatter | solution.py:159
  333.3 210.2 %reduce-scatter.25.cloned.1.call-start = ((), (), s32[]{:S(2)}) async-start(), calls=%async_computation.18 | async-start | bytes 3686400 | tf_op jit(solution)/shard_map/reduce_scatter | solution.py:159
  338.7 229.1 %reduce-scatter.45.cloned.1.call-start = ((), (), s32[]{:S(2)}) async-start(), calls=%async_computation.28 | async-start | bytes 819200
  338.8 4.4 copy-start.21
  338.8 4.6 copy-start.23
  343.4 4.2 copy-start.25
  346.4 33.0 %collective-permute-start.2 = (bf16[512,1280]{1,0:T(8,128)(2,1)}, bf16[512,1280]{1,0:T(8,128)(2,1)}, u32[]{:S(2)}, u32[]{:S(2)}) collective-permute-start(bf16[512,1280]{1,0:T(8,128)(2,1)} %fusion.4), channel_id=1, source_target_pairs={{1,0},{2,1},{3,2},{5,4},{6,5},{7,6},{9,8},{10,9},{11,10},{13,12},{... | collective-permute-start | bytes 3932168 | tf_op jit(solution)/shard_map/ppermute | solution.py:246
  354.5 236.6 %reduce-scatter.47.cloned.1.call-start = ((), (), s32[]{:S(2)}) async-start(), calls=%async_computation.29 | async-start | bytes 819200
  354.5 4.7 copy-start.22
  354.5 5.2 copy-start.24
  365.3 21.9 %copy-start.11 = (bf16[512,1280]{1,0:T(8,128)(2,1)S(1)}, bf16[512,1280]{1,0:T(8,128)(2,1)}, u32[]{:S(2)}) copy-start(bf16[512,1280]{1,0:T(8,128)(2,1)} %get-tuple-element.22) | copy-start | bytes 3932164
  365.3 249.0 %reduce-scatter.43.cloned.1.call-start = ((), (), s32[]{:S(2)}) async-start(), calls=%async_computation.27 | async-start | bytes 819200
  365.3 21.9 %copy-start.5 = (f32[512,1280]{1,0:T(8,128)S(1)}, f32[512,1280]{1,0:T(8,128)}, u32[]{:S(2)}) copy-start(f32[512,1280]{1,0:T(8,128)} %get-tuple-element.38) | copy-start | bytes 7864324
  385.9 59.2 %collective-permute-start.3 = (bf16[512,1280]{1,0:T(8,128)(2,1)}, bf16[512,1280]{1,0:T(8,128)(2,1)}, u32[]{:S(2)}, u32[]{:S(2)}) collective-permute-start(bf16[512,1280]{1,0:T(8,128)(2,1)} %add_convert_fusion), channel_id=1, source_target_pairs={{1,0},{2,1},{3,2},{5,4},{6,5},{7,6},{9,8},{10,9},{11,10},{13,12},{... | collective-permute-start | bytes 3932168 | tf_op jit(solution)/shard_map/ppermute | solution.py:246
  387.2 7.5 %copy-start.26 = (f32[1280]{0:T(1024)S(1)}, f32[1280]{0:T(1024)}, u32[]{:S(2)}) copy-start(f32[1280]{0:T(1024)} %param.23) | copy-start | bytes 15364
  394.6 242.9 %reduce-scatter.41.cloned.1.call-start = ((), (), s32[]{:S(2)}) async-start(), calls=%async_computation.26 | async-start | bytes 819200
  444.8 215.9 %reduce-scatter.39.cloned.1.call-start = ((), (), s32[]{:S(2)}) async-start(), calls=%async_computation.25 | async-start | bytes 819200
  495.2 188.8 %reduce-scatter.37.cloned.1.call-start = ((), (), s32[]{:S(2)}) async-start(), calls=%async_computation.24 | async-start | bytes 819200
  (4 other events, 7.0 us)
Sparse Core Ops, SparseCore 0:
  26.0 34.6 all-gather.14
  62.5 32.8 all-gather.16
  97.9 32.8 all-gather.12
  132.6 32.8 all-gather.18
  167.2 32.8 all-gather.20
  201.8 32.8 all-gather.22
  245.0 46.8 reduce-scatter.32
  295.3 46.8 reduce-scatter.34
  345.6 46.8 reduce-scatter.30
  395.8 46.8 reduce-scatter.28
  446.1 46.8 reduce-scatter.26
  496.3 47.0 reduce-scatter.24
  545.7 22.0 reduce-scatter.44
  570.0 21.0 reduce-scatter.46
  593.2 21.0 reduce-scatter.42
  616.4 21.0 reduce-scatter.40
  639.6 21.0 reduce-scatter.38
  662.9 21.0 reduce-scatter.36

commit v3 on v2

--- a/solution.py
+++ b/solution.py
@@ -149,16 +149,397 @@
         scratch_shapes=[pltpu.VMEM((features,rows),F32), pltpu.VMEM((width,rows),F32)],
         compiler_params=pltpu.CompilerParams(vmem_limit_bytes=60<<20), name="attend_backward")(q,k,kt,v,g,lse,delta,seg_q,seg_k)
 
-def gather_weight(block, row_axis, col_axis):
-    wide = lax.all_gather(block, "mp", axis=1 if col_axis == "mp" else 0, tiled=True)
-    return lax.all_gather(wide, "dp", axis=1 if col_axis == "dp" else 0, tiled=True)
-
-
-def scatter_grad(grad, row_axis, col_axis):
-    low = grad.astype(BF16)
-    mine = lax.psum_scatter(low, "dp", scatter_dimension=1 if col_axis == "dp" else 0, tiled=True)
-    mine = lax.psum_scatter(mine, "mp", scatter_dimension=1 if col_axis == "mp" else 0, tiled=True)
-    return mine.astype(F32)
+MESH = pl.DeviceIdType.MESH
+
+
+def bit_of(index, b):
+    return lax.rem(lax.div(index, 1 << b), 2)
+
+
+def flipped(index, bits):
+    for b in bits:
+        index = index + (1 << b) * (1 - 2 * bit_of(index, b))
+    return index
+
+
+def split_order(count, turn):
+    bits = list(range(count))
+    rest = bits[1:][::-1]
+    turn = turn % max(1, len(rest))
+    return bits[:1] + rest[turn:] + rest[:turn]
+
+
+def subsets(bits):
+    out = [()]
+    for b in bits:
+        out = out + [s + (b,) for s in out]
+    return out
+
+
+def greet(dp_bits, stages, extra=()):
+    d, z = lax.axis_index("dp"), lax.axis_index("mp")
+    barrier = pltpu.get_barrier_semaphore()
+    for b in range(dp_bits):
+        pl.semaphore_signal(barrier, device_id={"dp": flipped(d, (b,))}, device_id_type=MESH)
+    for step in range(1, stages):
+        pl.semaphore_signal(
+            barrier, device_id={"mp": lax.rem(z + step, stages)}, device_id_type=MESH
+        )
+    pl.semaphore_wait(barrier, dp_bits + stages - 1)
+    return d, z
+
+
+def gather_kernel(dp_bits, stages, back, *refs):
+    weights, refs = refs[:6], refs[6:]
+    bias, tokens, refs = refs[0], refs[1], refs[2:]
+    fulls, refs = refs[:6], refs[6:]
+    bias_all, window, refs = refs[0], refs[1], refs[2:]
+    blocks, slab, blank, zs, zr, ds, dr, ls, xs, xr, bs, br, blank_sem = refs
+    d, z = greet(dp_bits, stages)
+    cols = weights[0].shape[1]
+
+    def block_copy(w, step):
+        return pltpu.make_async_remote_copy(
+            src_ref=weights[w], dst_ref=blocks.at[w, step], send_sem=zs.at[w, step],
+            recv_sem=zr.at[w, step], device_id={"mp": lax.rem(z + step, stages)},
+            device_id_type=MESH,
+        )
+
+    def bias_copy(step):
+        return pltpu.make_async_remote_copy(
+            src_ref=bias, dst_ref=bias_all.at[step], send_sem=bs.at[step], recv_sem=br.at[step],
+            device_id={"mp": lax.rem(z + step, stages)}, device_id_type=MESH,
+        )
+
+    def token_copy(hop):
+        src = tokens if hop == 0 else window.at[hop - 1]
+        return pltpu.make_async_remote_copy(
+            src_ref=src, dst_ref=window.at[hop], send_sem=xs.at[hop], recv_sem=xr.at[hop],
+            device_id={"mp": jnp.minimum(z + 1, stages - 1)}, device_id_type=MESH,
+        )
+
+    sent = []
+    orders = [split_order(dp_bits, w)[::-1] for w in range(6)]
+
+    def slab_copy(w, at, held, b, slot):
+        which = flipped(d, held)
+        src = slab.at[w] if not held else fulls[w].at[which]
+        return pltpu.make_async_remote_copy(
+            src_ref=src, dst_ref=fulls[w].at[which], send_sem=ds.at[w, slot],
+            recv_sem=dr.at[w, which], device_id={"dp": flipped(d, (b,))}, device_id_type=MESH,
+        )
+
+    def slab_arrival(w, held, b, slot):
+        which = flipped(d, held + (b,))
+        return pltpu.make_async_remote_copy(
+            src_ref=slab.at[w], dst_ref=fulls[w].at[which], send_sem=ds.at[w, slot],
+            recv_sem=dr.at[w, which], device_id={"dp": flipped(d, (b,))}, device_id_type=MESH,
+        )
+
+    def start_blocks(w):
+        for step in range(1, stages):
+            copy = block_copy(w, step)
+            copy.start()
+            sent.append(copy)
+
+    def own_copy(w):
+        return pltpu.make_async_copy(slab.at[w], fulls[w].at[d], ls.at[w])
+
+    def finish_blocks(w):
+        blocks[w, 0] = weights[w][...]
+        for step in range(1, stages):
+            block_copy(w, step).wait_recv()
+        for me in range(stages):
+
+            @pl.when(z == me)
+            def _():
+                parts = [blocks[w, (me - s) % stages] for s in range(stages)]
+                slab[w] = jnp.concatenate(parts, axis=1)
+
+        own_copy(w).start()
+
+    def start_round(w, k):
+        order = orders[w]
+        for slot, held in enumerate(subsets(order[:k])):
+            copy = slab_copy(w, d, held, order[k], (1 << k) - 1 + slot)
+            copy.start()
+            sent.append(copy)
+
+    def finish_round(w, k):
+        order = orders[w]
+        for slot, held in enumerate(subsets(order[:k])):
+            slab_arrival(w, held, order[k], (1 << k) - 1 + slot).wait_recv()
+
+    for w in range(3):
+        start_blocks(w)
+    for step in range(1, stages):
+        copy = bias_copy(step)
+        copy.start()
+        sent.append(copy)
+
+    @pl.when(z < stages - 1)
+    def _():
+        token_copy(0).start()
+
+    for w in range(3, 6):
+        start_blocks(w)
+    blank[...] = jnp.zeros_like(blank)
+    bias_all[0] = bias[...]
+
+    def blank_copy(hop):
+        return pltpu.make_async_copy(blank, window.at[hop], blank_sem.at[hop])
+
+    for hop in range(back):
+
+        @pl.when(z <= hop)
+        def _():
+            blank_copy(hop).start()
+
+    for w in range(3):
+        finish_blocks(w)
+        start_round(w, 0)
+    for k in range(1, dp_bits):
+        for w in range(3):
+            finish_round(w, k - 1)
+            start_round(w, k)
+    for hop in range(back):
+
+        @pl.when(z > hop)
+        def _():
+            token_copy(hop).wait_recv()
+
+        if hop + 1 < back:
+
+            @pl.when((z > hop) & (z < stages - 1))
+            def _():
+                token_copy(hop + 1).start()
+
+    for w in range(3, 6):
+        finish_blocks(w)
+        start_round(w, 0)
+    for k in range(1, dp_bits):
+        for w in range(3, 6):
+            finish_round(w, k - 1)
+            start_round(w, k)
+    for w in range(6):
+        finish_round(w, dp_bits - 1)
+        own_copy(w).wait()
+    for step in range(1, stages):
+        bias_copy(step).wait_recv()
+    for hop in range(back):
+
+        @pl.when((z >= hop) & (z < stages - 1))
+        def _():
+            token_copy(hop).wait_send()
+
+        @pl.when(z <= hop)
+        def _():
+            blank_copy(hop).wait()
+
+    for copy in sent:
+        copy.wait_send()
+
+
+def gather_all(weights, bias, tokens, dp, stages, back):
+    rows, cols = weights[0].shape
+    held, features = tokens.shape
+    dp_bits = dp.bit_length() - 1
+    hbm = pl.BlockSpec(memory_space=pl.ANY)
+    vmem = pl.BlockSpec(memory_space=pltpu.VMEM)
+    dma = pltpu.SemaphoreType.DMA
+    out = pl.pallas_call(
+        functools.partial(gather_kernel, dp_bits, stages, back),
+        in_specs=[vmem] * 7 + [hbm],
+        out_specs=[hbm] * 6 + [vmem, hbm],
+        out_shape=[jax.ShapeDtypeStruct((dp, rows, cols * stages), BF16)] * 6
+        + [
+            jax.ShapeDtypeStruct((stages,) + bias.shape, F32),
+            jax.ShapeDtypeStruct((back, held, features), BF16),
+        ],
+        scratch_shapes=[
+            pltpu.VMEM((6, stages, rows, cols), BF16),
+            pltpu.VMEM((6, rows, cols * stages), BF16),
+            pltpu.VMEM((held, features), BF16),
+            dma((6, stages)), dma((6, stages)), dma((6, dp)), dma((6, dp)), dma((6,)),
+            dma((back,)), dma((back,)), dma((stages,)), dma((stages,)), dma((back,)),
+        ],
+        compiler_params=pltpu.CompilerParams(
+            collective_id=0, has_side_effects=True, vmem_limit_bytes=40 << 20
+        ),
+        name="gather_all",
+    )(*weights, bias, tokens)
+    fulls = [f.reshape(dp * rows, cols * stages) for f in out[:6]]
+    return fulls, out[6], out[7]
+
+
+def add_into(dst, src, count, chunk):
+    rows = dst.shape[1]
+
+    def step(index, carry):
+        i, at = index // (rows // chunk), lax.rem(index, rows // chunk)
+        at = pl.ds(pl.multiple_of(at * chunk, chunk), chunk)
+        dst[i, at, :] = (dst[i, at, :].astype(F32) + src(i, at).astype(F32)).astype(BF16)
+        return carry
+
+    lax.fori_loop(0, count * (rows // chunk), step, 0)
+
+
+def reduce_kernel(dp_bits, stages, *refs):
+    grads, refs = refs[:6], refs[6:]
+    sums, refs = refs[0], refs[1:]
+    outs, refs = refs[:6], refs[6:]
+    total, refs = refs[0], refs[1:]
+    kept, got = refs[0], refs[1 : 1 + dp_bits]
+    zsend, zgot, sgot, ks, rs, rr, zs, zr, ss, sr = refs[1 + dp_bits :]
+    d, z = greet(dp_bits, stages)
+    half = 1 << (dp_bits - 1)
+    rows, features = kept.shape[2], kept.shape[3]
+    chunk = 32 if rows % 32 == 0 else 8
+    orders = [split_order(dp_bits, w) for w in range(6)]
+    sent = []
+
+    def place(w, slot, low):
+        rest = orders[w][1:]
+        at = low
+        for i, b in enumerate(rest):
+            if slot >> (len(rest) - 1 - i) & 1:
+                at = at + (1 << b)
+        return at
+
+    def first_copy(w, slot):
+        return pltpu.make_async_remote_copy(
+            src_ref=grads[w].at[place(w, slot, 1 - bit_of(d, 0))], dst_ref=got[0].at[w, slot],
+            send_sem=rs.at[w, slot], recv_sem=rr.at[w, slot],
+            device_id={"dp": flipped(d, (0,))}, device_id_type=MESH,
+        )
+
+    def keep_copy(w, slot):
+        return pltpu.make_async_copy(
+            grads[w].at[place(w, slot, bit_of(d, 0))], kept.at[w, slot], ks.at[w, slot]
+        )
+
+    def round_copy(w, k):
+        count = half >> k
+        b = orders[w][k]
+        other = 1 - bit_of(d, b)
+        return pltpu.make_async_remote_copy(
+            src_ref=got[k - 1].at[w, pl.ds(other * count, count)], dst_ref=got[k].at[w],
+            send_sem=rs.at[w, half + k], recv_sem=rr.at[w, half + k],
+            device_id={"dp": flipped(d, (b,))}, device_id_type=MESH,
+        )
+
+    def last_copy(w, step):
+        to = lax.rem(z + step, stages)
+        return pltpu.make_async_remote_copy(
+            src_ref=zsend.at[w, to], dst_ref=zgot.at[w, step], send_sem=zs.at[w, step],
+            recv_sem=zr.at[w, step], device_id={"mp": to}, device_id_type=MESH,
+        )
+
+    def sum_copy(k):
+        if k < dp_bits:
+            to = {"dp": flipped(d, (k,))}
+        else:
+            to = {"mp": flipped(z, (k - dp_bits,))}
+        return pltpu.make_async_remote_copy(
+            src_ref=total.at[k], dst_ref=sgot.at[k], send_sem=ss.at[k], recv_sem=sr.at[k],
+            device_id=to, device_id_type=MESH,
+        )
+
+    def start(copy):
+        copy.start()
+        sent.append(copy)
+
+    def begin_first(w):
+        for slot in range(half):
+            start(first_copy(w, slot))
+            keep_copy(w, slot).start()
+
+    def finish_first(w):
+        for slot in range(half):
+            keep_copy(w, slot).wait()
+            first_copy(w, slot).wait_recv()
+        add_into(got[0].at[w], lambda i, at: kept[w, i, at, :], half, chunk)
+
+    def finish_round(w, k):
+        count = half >> k
+        round_copy(w, k).wait_recv()
+        mine = bit_of(d, orders[w][k]) * count
+        add_into(got[k].at[w], lambda i, at: got[k - 1][w, mine + i, at, :], count, chunk)
+
+    def begin_last(w):
+        cols = features // stages
+        for s in range(stages):
+            zsend[w, s] = got[dp_bits - 1][w, 0, :, s * cols : (s + 1) * cols]
+        for step in range(1, stages):
+            start(last_copy(w, step))
+
+    def finish_last(w):
+        value = zsend[w, z].astype(F32)
+        for step in range(1, stages):
+            last_copy(w, step).wait_recv()
+            value = value + zgot[w, step].astype(F32)
+        outs[w][...] = value
+
+    levels = dp_bits + stages.bit_length() - 1
+    total[0] = sums[...]
+    start(sum_copy(0))
+    for w in range(6):
+        begin_first(w)
+
+    def sum_step(k):
+        sum_copy(k).wait_recv()
+        total[k + 1] = total[k] + sgot[k]
+        if k + 1 < levels:
+            start(sum_copy(k + 1))
+
+    for w in range(6):
+        finish_first(w)
+        start(round_copy(w, 1)) if dp_bits > 1 else begin_last(w)
+        if w < levels:
+            sum_step(w)
+    for k in range(6, levels):
+        sum_step(k)
+    for k in range(1, dp_bits):
+        for w in range(6):
+            finish_round(w, k)
+            start(round_copy(w, k + 1)) if k + 1 < dp_bits else begin_last(w)
+    for w in range(6):
+        finish_last(w)
+    for copy in sent:
+        copy.wait_send()
+
+
+def reduce_all(grads, sums, dp, stages):
+    features = grads[0].shape[1]
+    rows, cols = grads[0].shape[0] // dp, features // stages
+    dp_bits = dp.bit_length() - 1
+    half = dp // 2
+    levels = dp_bits + stages.bit_length() - 1
+    hbm = pl.BlockSpec(memory_space=pl.ANY)
+    vmem = pl.BlockSpec(memory_space=pltpu.VMEM)
+    dma = pltpu.SemaphoreType.DMA
+    lines = sums.shape[0]
+    out = pl.pallas_call(
+        functools.partial(reduce_kernel, dp_bits, stages),
+        in_specs=[hbm] * 6 + [vmem],
+        out_specs=[vmem] * 7,
+        out_shape=[jax.ShapeDtypeStruct((rows, cols), F32)] * 6
+        + [jax.ShapeDtypeStruct((levels + 1, lines, LANES), F32)],
+        scratch_shapes=[pltpu.VMEM((6, half, rows, features), BF16)]
+        + [pltpu.VMEM((6, half >> k, rows, features), BF16) for k in range(dp_bits)]
+        + [
+            pltpu.VMEM((6, stages, rows, cols), BF16),
+            pltpu.VMEM((6, stages, rows, cols), BF16),
+            pltpu.VMEM((levels, lines, LANES), F32),
+            dma((6, half)), dma((6, half + dp_bits)), dma((6, half + dp_bits)),
+            dma((6, stages)), dma((6, stages)), dma((levels,)), dma((levels,)),
+        ],
+        compiler_params=pltpu.CompilerParams(
+            collective_id=1, has_side_effects=True, vmem_limit_bytes=56 << 20
+        ),
+        name="reduce_all",
+    )(*[g.reshape(dp, rows, features) for g in grads], sums)
+    return out[:6], out[6][levels]
 
 
 def body(
@@ -175,19 +556,19 @@
     up = [(i, i + 1) for i in range(stages - 1)]
     down = [(i + 1, i) for i in range(stages - 1)]
 
-    wq, wk, wv, wu = (
-        gather_weight(w, "dp", "mp") for w in (w_query, w_key, w_value, w_up)
-    )
-    wo, wd = (gather_weight(w, "mp", "dp") for w in (w_output, w_down))
-    b_full = lax.all_gather(b_up, "mp", axis=0, tiled=True)
+    (wq, wk, wv, wu, wo, wd), b_all, before = gather_all(
+        (w_query, w_key, w_value, w_up, w_output.T, w_down.T), b_up[None], tokens,
+        lax.axis_size("dp"), stages, back,
+    )
+    b_full = b_all[(z - jnp.arange(stages)) % stages].reshape(-1)
 
     inputs = tokens.astype(F32)
     inv_first = row_inverse(inputs)
     normed = (inputs * inv_first * gain_attn).astype(BF16)
-    window = [normed]
-    for _ in range(back):
-        window.append(lax.ppermute(window[-1], "mp", up))
-    first = jnp.concatenate(window[::-1], axis=0)
+    others = before[::-1].reshape(own, features).astype(F32)
+    first = jnp.concatenate(
+        [(others * row_inverse(others) * gain_attn).astype(BF16), normed], axis=0
+    )
 
     seg_wide = jnp.concatenate([jnp.full((own,), -1, jnp.int32), seg])
     seg_window = lax.dynamic_slice_in_dim(seg_wide, z * rows, own + rows, 0)
@@ -203,16 +584,16 @@
     values = jnp.dot(first, wv, preferred_element_type=F32).astype(BF16)
     mixed, lse = attend_forward(scaled, keys, values.T, seg_query, seg_key, block)
 
-    hidden = inputs + jnp.dot(mixed, wo, preferred_element_type=F32)
+    hidden = inputs + dot(mixed, wo, 1, 1)
     inv_second = row_inverse(hidden)
     second = (hidden * inv_second * gain_mlp).astype(BF16)
     preact = jnp.dot(second, wu, preferred_element_type=F32) + b_full
     active = jax.nn.silu(preact).astype(BF16)
-    layer_out = (hidden + jnp.dot(active, wd, preferred_element_type=F32) + b_down).astype(BF16)
+    layer_out = (hidden + dot(active, wd, 1, 1) + b_down).astype(BF16)
 
     upstream = cotangent.astype(F32)
     sigma = jax.nn.sigmoid(preact)
-    d_active = dot(cotangent, wd, 1, 1)
+    d_active = dot(cotangent, wd, 1, 0)
     d_preact = (d_active * sigma * (1.0 + preact * (1.0 - sigma))).astype(BF16)
     d_second = dot(d_preact, wu, 1, 1)
     weighted = d_second * gain_mlp
@@ -220,7 +601,7 @@
     cube = inv_second * inv_second * inv_second
     d_hidden = upstream + inv_second * weighted - hidden * cube / features * dots
     d_attn = d_hidden.astype(BF16)
-    d_mixed = dot(d_attn, wo, 1, 1).astype(BF16)
+    d_mixed = dot(d_attn, wo, 1, 0).astype(BF16)
 
     owner = (jnp.arange(features)[None, :] // HD == jnp.arange(heads)[:, None]).astype(F32)
     delta = lax.dot_general(
@@ -259,7 +640,20 @@
     sums = jnp.concatenate(
         [grad_gain_mlp, jnp.sum(upstream, axis=0), grad_b_up, grad_gain_attn, scale_part]
     )
-    sums = lax.psum(sums, ("dp", "mp"))
+    lines = -(-sums.shape[0] // (8 * LANES)) * 8
+    grads, sums = reduce_all(
+        [
+            dot(normed, d_query, 0, 0).astype(BF16),
+            dot(first, d_keys, 0, 0).astype(BF16),
+            dot(first, d_values, 0, 0).astype(BF16),
+            dot(second, d_preact, 0, 0).astype(BF16),
+            dot(d_attn, mixed, 0, 0).astype(BF16),
+            dot(cotangent, active, 0, 0).astype(BF16),
+        ],
+        jnp.pad(sums, (0, lines * LANES - sums.shape[0])).reshape(lines, LANES),
+        lax.axis_size("dp"), stages,
+    )
+    sums = sums.reshape(-1)[: 4 * features + HD]
     sum_gain_mlp, sum_b_down, sum_b_up, sum_gain_attn, scale_total = jnp.split(
         sums, [features, 2 * features, 3 * features, 4 * features]
     )
@@ -267,17 +661,9 @@
     sum_b_up = lax.dynamic_slice_in_dim(sum_b_up, z * mine, mine, 0)
     grad_query_scale = scale_total * (LOG2E / math.sqrt(HD)) * jax.nn.sigmoid(query_scale)
 
-    grads = (
-        scatter_grad(dot(normed, d_query, 0, 0), "dp", "mp"),
-        scatter_grad(dot(first, d_keys, 0, 0), "dp", "mp"),
-        scatter_grad(dot(first, d_values, 0, 0), "dp", "mp"),
-        scatter_grad(dot(mixed, d_attn, 0, 0), "mp", "dp"),
-        scatter_grad(dot(second, d_preact, 0, 0), "dp", "mp"),
-        scatter_grad(dot(active, cotangent, 0, 0), "mp", "dp"),
-    )
     return (
-        layer_out, tokens_grad, grads[0], grads[1], grads[2], grads[3], grads[4], sum_b_up,
-        grads[5], sum_b_down, sum_gain_attn, sum_gain_mlp, grad_query_scale,
+        layer_out, tokens_grad, grads[0], grads[1], grads[2], grads[4].T, grads[3], sum_b_up,
+        grads[5].T, sum_b_down, sum_gain_attn, sum_gain_mlp, grad_query_scale,
     )
 
 

time: 702 us -> 569 us (0.81)
  Pallas kernels: 70.1 us -> 351 us
  waiting for transfers between devices: 233 us -> 58.3 us
  blocking collectives: 169 us -> 0 us
  matrix products: 133 us -> 95.3 us
  between operations: 16 us -> 1.4 us
  starting transfers between devices: 12.7 us -> 2.73 us
    pallas_call x0 -> x2, Pallas kernels: none -> 281 us  [the longest x1 147 us: reduce_all(): pl.pallas_call(functools.partial(reduce_kernel, dp_bits, stages), in_spec...]
    unnamed x24 -> x0, waiting for transfers between devices: 125 us -> none
    all_gather x6 -> x0, blocking collectives: 112 us -> none  [gather_weight(): lax.all_gather(block, 'mp', axis=1 if col_axis == 'mp' else 0, tiled=True)]
    reduce_scatter x6 -> x0, waiting for transfers between devices: 93.9 us -> none  [scatter_grad(): lax.psum_scatter(low, 'dp', scatter_dimension=1 if col_axis == 'dp' else...]
    ppermute x2, waiting for transfers between devices: 14.1 us -> 58.3 us  [body(): part = lax.ppermute(term.astype(BF16), 'mp', down).astype(F32)]
    psum x1 -> x0, blocking collectives: 39.6 us -> none  [body(): sums = lax.psum(sums, ('dp', 'mp'))]
    unnamed x1 -> x0, blocking collectives: 17.8 us -> none
    dot_general x16 -> x18, matrix products: 85.9 us -> 69.5 us  [dot(): lax.dot_general(a, b, (((ca,), (cb,)), ((), ())), preferred_element_type=...]
  transfers between devices with their start and end apart: 22 -> 2, of which waited for: 11 -> 2; matrix products, arithmetic and copies ran while one was open for 25% -> 8% of each run, Pallas kernels for 10% -> 0%
where the time goes in v3:
time: 569 us; the launch traced here: 563 us
  Pallas kernels  351 us (62%)
  matrix products  95.3 us (17%)
  waiting for transfers between devices  58.3 us (10%)
  local copies, waits for them, and re-layouts  40.6 us (7%)
  other arithmetic  13.9 us (2%)
    pallas_call x1, Pallas kernels, reduce_all(): pl.pallas_call(functools.partial(reduce_kernel, dp_bits, stages), in_spec...  147 us
    pallas_call x1, Pallas kernels, gather_all(): pl.pallas_call(functools.partial(gather_kernel, dp_bits, stages, back), i...  133 us
    dot_general x18, matrix products, dot(): lax.dot_general(a, b, (((ca,), (cb,)), ((), ())), preferred_element_type=...  69.5 us
    ppermute x2, waiting for transfers between devices, body(): part = lax.ppermute(term.astype(BF16), 'mp', down).astype(F32)  58.3 us
    pallas_call x1, Pallas kernels, attend_backward(): pl.pallas_call(functools.partial(backward_kernel, block), out_shape=[jax....  44.9 us
    pallas_call x1, Pallas kernels, attend_forward(): pl.pallas_call(functools.partial(forward_kernel, block), out_shape=[jax.S...  25.1 us
    unnamed x122, local copies, waits for them, and re-layouts  21.3 us
  transfers between devices with their start and end apart: 2, of which 2 were waited for; matrix products, arithmetic and copies ran while one was open for 8% of the time, Pallas kernels for 0%

profile of v3, /device:TPU:0, one launch (start us, length us, event | category | flops | bytes accessed | tf_op | source)
XLA Modules:
  0.0 562.9 jit_solution(1408745196828351934)
XLA Ops:
  1.3 1.6 fusion.11
  3.0 1.3 copy-done
  4.3 0.9 copy-done.2
  5.2 0.9 copy-done.3
  7.0 0.9 copy-done.5
  9.7 133.3 %gather_all.1 = (bf16[8,160,1280]{2,1,0:T(8,128)(2,1)S(1)}, bf16[8,160,1280]{2,1,0:T(8,128)(2,1)S(1)}, bf16[8,160,1280]{2,1,0:T(8,128)(2,1)S(1)}, bf16[8,160,128...) custom-call(bf16[160,320]{1,0:T(8,128)(2,1)S(1)} %copy-done.2, ...), custom_call_target="tpu_custom_call" | custom-call | tf_op jit(solution)/shard_map/gather_all/pallas_call | solution.py:350
  143.1 1.7 copy-done.8
  144.8 1.8 copy-done.10
  146.6 1.6 copy-done.14
  148.8 2.7 reverse_convert_fusion
  152.4 1.2 broadcast_in_dim.9.seg_key
  154.7 3.5 fusion.1
  158.6 8.0 %convolution_convert_fusion.6.v_ref = bf16[1536,1280]{1,0:T(8,128)(2,1)} fusion(bf16[1280,1280]{1,0:T(8,128)(2,1)S(1)} %bitcast.86, bf16[512,1280]{1,0:T(8,128)(2,1)S(1)} %fusion.13, bf16[1024,1280]{1,0:T(8,128)(2,1)S(1)} %fusion.1), kind=kOutput, calls=%fused_computation.7 | convolution fusion | flops 5042995200 | bytes 11141120 | tf_op jit(solution)/shard_map/dot_general | solution.py:584
  166.6 7.9 %convolution_convert_fusion.7 = bf16[1536,1280]{0,1:T(8,128)(2,1)} fusion(bf16[1280,1280]{1,0:T(8,128)(2,1)S(1)} %bitcast.91, bf16[512,1280]{1,0:T(8,128)(2,1)S(1)} %fusion.13, bf16[1024,1280]{1,0:T(8,128)(2,1)S(1)} %fusion.1), kind=kOutput, calls=%fused_computation.8 | convolution fusion | flops 5042995200 | bytes 11141120 | tf_op jit(solution)/shard_map/dot_general | solution.py:583
  174.6 6.2 %copy.38.k_ref = bf16[1536,1280]{1,0:T(8,128)(2,1)} copy(bf16[1536,1280]{0,1:T(8,128)(2,1)} %convolution_convert_fusion.7) | data formatting | bytes 7864320 | tf_op jit(solution)/shard_map/convert_element_type | solution.py:583
  180.7 6.3 %copy.39.vt_ref = bf16[1280,1536]{1,0:T(8,128)(2,1)} copy(bf16[1280,1536]{0,1:T(8,128)(2,1)} %bitcast.94) | data formatting | bytes 7864320 | tf_op jit(solution)/shard_map/convert_element_type | solution.py:584
  187.0 5.7 %multiply_convert_fusion.2 = (bf16[512,1280]{1,0:T(8,128)(2,1)}, f32[512,1280]{1,0:T(8,128)}) fusion(f32[1280]{0:T(1024)S(1)} %mul.230, bf16[512,1280]{1,0:T(8,128)(2,1)S(1)} %fusion.13, bf16[1280,1280]{1,0:T(8,128)(2,1)} %bitcast.84), kind=kOutput, calls=%fused_computation.64 | convolution fusion | flops 1679032320 | bytes 8524800 | tf_op jit(solution)/shard_map/dot_general | solution.py:581
  192.7 25.1 %attend_forward.1 = (bf16[512,1280]{1,0:T(8,128)(2,1)}, f32[16,512]{1,0:T(8,128)}) custom-call(bf16[512,1280]{1,0:T(8,128)(2,1)} %get-tuple-element.67.q_ref, bf16[1536,1280]{1,0:T(8,128)(2,1)} %copy.38.k_ref, bf16[1280,1536]{1,0:T(8,128)(2,1)} %copy.39.vt_ref, s32[1,512]{1,0:T(1,128)} %bitcast.107, s32[1536,1]{1,0:T(8,128)} %broadcast_in_dim.9.seg_key), custom_call_target="tpu_custom_call" | custom-call | tf_op jit(solution)/shard_map/attend_forward/pallas_call | solution.py:107
  217.8 3.5 multiply_reduce_fusion.3
  221.4 1.9 convolution_add_fusion.5
  223.6 1.8 copy-done.45
  225.4 2.4 convert_reduce_fusion.1
  227.8 2.2 multiply_reduce_fusion.1
  230.8 1.9 convolution_convert_fusion.8.g_ref
  233.1 2.1 fusion.20.delta_ref
  235.2 44.9 %attend_backward.1 = (bf16[512,1280]{1,0:T(8,128)(2,1)}, bf16[1536,1280]{1,0:T(8,128)(2,1)}, bf16[1536,1280]{1,0:T(8,128)(2,1)}) custom-call(bf16[512,1280]{1,0:T(8,128)(2,1)} %get-tuple-element.67.q_ref, bf16[1536,1280]{1,0:T(8,128)(2,1)} %copy.38.k_ref, bf16[1280,1536]{1,0:T(8,128)(2,1)} %bitcast.95, bf16[1536,1280]{1,0:T(8,128)(2,1)} %convolution_convert_fusion.6.v_ref, ...), custom_call_target="tpu_custom_call" | custom-call | tf_op jit(solution)/shard_map/attend_backward/pallas_call | solution.py:147
  280.2 4.4 fusion.25
  284.6 2.9 fusion.7
  287.6 1.5 collective-permute-start
  289.1 6.0 %convolution_convert_fusion.2 = bf16[1280,1280]{1,0:T(8,128)(2,1)} fusion(bf16[512,1280]{1,0:T(8,128)(2,1)} %copy-done.54, f32[512,1280]{1,0:T(8,128)} %copy-done.21, f32[1280]{0:T(1024)S(1)} %copy-done.41, f32[512]{0:T(512)S(1)} %get-tuple-element.66), kind=kOutput, calls=%fused_computation.3 | convolution fusion | flops 1681326080 | bytes 7216128 | tf_op jit(solution)/shard_map/dot_general | solution.py:22
  295.1 3.7 convolution_convert_fusion
  298.8 3.7 convolution_convert_fusion.1
  302.5 1.9 fusion.30
  304.5 1.9 fusion.33
  307.2 3.3 fusion.6
  310.5 3.4 convolution_add_fusion.3
  313.8 3.9 convolution_convert_fusion.5
  318.1 1.4 copy-done.24
  319.4 7.0 %convolution_convert_fusion.3 = bf16[1280,1280]{1,0:T(8,128)(2,1)} fusion(bf16[1536,1280]{1,0:T(8,128)(2,1)S(1)} %copy-done.44, bf16[512,1280]{1,0:T(8,128)(2,1)S(1)} %copy-done.30, bf16[1024,1280]{1,0:T(8,128)(2,1)S(1)} %copy-done.24), kind=kOutput, calls=%fused_computation.4 | convolution fusion | flops 5042667520 | bytes 11141120 | tf_op jit(solution)/shard_map/dot_general | solution.py:22
  326.4 1.1 collective-permute-done
  327.6 4.3 add_convert_fusion
  331.8 1.3 collective-permute-start.1
  333.3 9.5 %convolution_convert_fusion.4 = bf16[1280,1280]{1,0:T(8,128)(2,1)} fusion(bf16[1536,1280]{1,0:T(8,128)(2,1)} %get-tuple-element.43, bf16[512,1280]{1,0:T(8,128)(2,1)S(1)} %copy-done.30, bf16[1024,1280]{1,0:T(8,128)(2,1)} %copy-done.23), kind=kOutput, calls=%fused_computation.5 | convolution fusion | flops 5042667520 | bytes 11141120 | tf_op jit(solution)/shard_map/dot_general | solution.py:22
  342.8 57.1 %collective-permute-done.1 = bf16[512,1280]{1,0:T(8,128)(2,1)} collective-permute-done((bf16[512,1280]{1,0:T(8,128)(2,1)}, bf16[512,1280]{1,0:T(8,128)(2,1)}, u32[]{:S(2)}, u32[]{:S(2)}) %collective-permute-start.1) | collective-permute-done | bytes 1310752 | tf_op jit(solution)/shard_map/ppermute | solution.py:627
  400.0 3.8 fusion.19
  404.4 147.4 %reduce_all.1 = (f32[160,320]{1,0:T(8,128)}, f32[160,320]{1,0:T(8,128)}, f32[160,320]{1,0:T(8,128)}, f32[160,320]{1,0:T(8,128)}, f32[160,320]{1,0:T(8,128)}, /*index=5*/f32[160,320]{1,0:T(8,128)}, f32[6,48,128]{2,1,0:T(8,128)}) custom-call(bf16[8,160,1280]{2,1,0:T(8,128)(2,1)} %bitcast.99, bf16[8,160,1280]{2,1,0:T(8,128)(2,1)} %bitcast.101, ...), custom_call_target="tpu_custom_call" | custom-call | tf_op jit(solution)/shard_map/reduce_all/pallas_call | solution.py:522
  552.5 1.4 slice_bitcast_fusion.1
  555.2 3.3 fusion.16
  (141 shorter events, 16.0 us)
Async XLA Ops:
  144.8 1.8 copy-start.10
  148.8 2.8 copy-start.50
  148.8 2.8 copy-start.40
  148.8 5.5 copy-start.1
  148.8 5.5 copy-start.39
  154.7 32.3 %copy-start.29 = (bf16[512,1280]{1,0:T(8,128)(2,1)}, bf16[512,1280]{1,0:T(8,128)(2,1)S(1)}, u32[]{:S(2)}) copy-start(bf16[512,1280]{1,0:T(8,128)(2,1)S(1)} %fusion.13) | copy-start | bytes 3932164
  154.7 4.0 copy-start.11
  158.2 8.4 %copy-start.23 = (bf16[1024,1280]{1,0:T(8,128)(2,1)}, bf16[1024,1280]{1,0:T(8,128)(2,1)S(1)}, u32[]{:S(2)}) copy-start(bf16[1024,1280]{1,0:T(8,128)(2,1)S(1)} %fusion.1) | copy-start | bytes 7864324
  158.6 8.0 %copy-start.15 = (bf16[8,160,1280]{2,1,0:T(8,128)(2,1)S(1)}, bf16[8,160,1280]{2,1,0:T(8,128)(2,1)}, u32[]{:S(2)}) copy-start(bf16[8,160,1280]{2,1,0:T(8,128)(2,1)} %copy-done.14) | copy-start | bytes 9830404
  192.7 25.1 %copy-start.47 = (bf16[8,160,1280]{2,1,0:T(8,128)(2,1)S(1)}, bf16[8,160,1280]{2,1,0:T(8,128)(2,1)}, u32[]{:S(2)}) copy-start(bf16[8,160,1280]{2,1,0:T(8,128)(2,1)} %get-tuple-element.38) | copy-start | bytes 9830404
  217.8 3.5 copy-start.41
  217.8 3.5 copy-start.48
  221.3 8.7 %copy-start.21 = (f32[512,1280]{1,0:T(8,128)}, f32[512,1280]{1,0:T(8,128)S(1)}, u32[]{:S(2)}) copy-start(f32[512,1280]{1,0:T(8,128)S(1)} %get-tuple-element.70) | copy-start | bytes 7864324
  221.4 2.2 copy-start.26
  221.4 4.0 copy-start.45
  223.3 4.5 copy-start.52
  227.8 2.2 copy-start.54
  230.8 1.9 copy-start.17
  230.8 2.3 copy-start.27
  233.1 2.1 copy-start.20
  280.1 4.4 copy-start.12
  280.2 4.5 copy-start.43
  287.6 40.0 %collective-permute-start = (bf16[512,1280]{1,0:T(8,128)(2,1)}, bf16[512,1280]{1,0:T(8,128)(2,1)}, u32[]{:S(2)}, u32[]{:S(2)}) collective-permute-start(bf16[512,1280]{1,0:T(8,128)(2,1)} %fusion.7), channel_id=1, source_target_pairs={{1,0},{2,1},{3,2},{5,4},{6,5},{7,6},{9,8},{10,9},{11,10},{13,12},{... | collective-permute-start | bytes 3932168 | tf_op jit(solution)/shard_map/ppermute | solution.py:627
  289.1 6.0 %copy-start.53 = (f32[512,1280]{1,0:T(8,128)S(1)}, f32[512,1280]{1,0:T(8,128)}, u32[]{:S(2)}) copy-start(f32[512,1280]{1,0:T(8,128)} %copy-done.52) | copy-start | bytes 7864324
  295.1 3.7 copy-start.18
  295.1 3.7 copy-start.28
  298.8 3.7 copy-start.16
  298.8 3.7 copy-start.42
  304.4 1.9 copy-start.22
  304.4 2.7 copy-start.46
  304.4 2.7 copy-start.49
  307.1 3.3 copy-start.13
  307.1 3.3 copy-start.44
  310.5 3.4 copy-start.30
  310.5 3.4 copy-start.31
  313.8 3.9 copy-start.25
  317.7 1.7 copy-start.24
  331.8 68.1 %collective-permute-start.1 = (bf16[512,1280]{1,0:T(8,128)(2,1)}, bf16[512,1280]{1,0:T(8,128)(2,1)}, u32[]{:S(2)}, u32[]{:S(2)}) collective-permute-start(bf16[512,1280]{1,0:T(8,128)(2,1)} %add_convert_fusion), channel_id=1, source_target_pairs={{1,0},{2,1},{3,2},{5,4},{6,5},{7,6},{9,8},{10,9},{11,10},{13,12},{... | collective-permute-start | bytes 3932168 | tf_op jit(solution)/shard_map/ppermute | solution.py:627
  333.3 66.7 %copy-start.9 = (bf16[8,160,1280]{2,1,0:T(8,128)(2,1)S(1)}, bf16[8,160,1280]{2,1,0:T(8,128)(2,1)}, u32[]{:S(2)}) copy-start(bf16[8,160,1280]{2,1,0:T(8,128)(2,1)} %copy-done.8) | copy-start | bytes 9830404
  333.3 66.7 %copy-start.32 = (bf16[512,1280]{1,0:T(8,128)(2,1)S(1)}, bf16[512,1280]{1,0:T(8,128)(2,1)}, u32[]{:S(2)}) copy-start(bf16[512,1280]{1,0:T(8,128)(2,1)} %get-tuple-element.45) | copy-start | bytes 3932164
  333.3 66.7 %copy-start.51 = (f32[512,1280]{1,0:T(8,128)S(1)}, f32[512,1280]{1,0:T(8,128)}, u32[]{:S(2)}) copy-start(f32[512,1280]{1,0:T(8,128)} %convolution_add_fusion.3) | copy-start | bytes 7864324
  404.4 150.8 %copy-start.19 = (f32[512,1280]{1,0:T(8,128)S(1)}, f32[512,1280]{1,0:T(8,128)}, u32[]{:S(2)}) copy-start(f32[512,1280]{1,0:T(8,128)} %copy-done.17) | copy-start | bytes 7864324
  555.2 3.3 copy-start.38
  555.2 4.0 copy-start.37
  555.2 4.7 copy-start.36
  555.2 5.4 copy-start.35
  555.2 6.1 %copy-start.34 = (f32[160,320]{1,0:T(8,128)S(1)}, f32[160,320]{1,0:T(8,128)}, u32[]{:S(2)}) copy-start(f32[160,320]{1,0:T(8,128)} %get-tuple-element.94) | copy-start | bytes 614404
  558.5 3.5 copy-start.33
  (9 other events, 10.1 us)
